TPU v7x, 1024 devices: a whole 8x8x8 slice. The times are simulated.
1024 devices in a mesh: cells: 128 (over z, y, core), states: 8 (over x).
Axes of the slice: x: 8, y: 8, z: 8, core: 2. Of those that a mesh axis runs over, the one named last changes fastest.
Arguments:
- filter_input: bfloat16 [81536, 1024], P('cells', 'states'), may hold values from -4 to 4, as said below
- cell_table: bfloat16 [8, 343, 343], replicated, may hold values from -0.5 to 3.5, as said below
- cell_type: int32 [256], P('cells'), may hold values from 0 to 7
- atom_center: int32 [512], P('cells'), may hold values from 0 to 1, as said below
- proj_values: bfloat16 [512, 3, 16, 343], P('cells'), may hold values from -0.3125 to 0.3125
- coupling: float32 [16, 16], replicated, may hold values from -1.5 to 1.5
- occupation: float32 [1024], P('states'), may hold values from 0.25 to 4
Outputs:
- filtered: float32 [81536, 1024], P('cells', 'states')
- density: float32 [81536], P('cells')
Inputs may be any that keep to these rules, and one draw needn't show every extreme that they name: `filter_input`: rows that stand for the same node on two blocks hold the same values. `cell_table`: each of the 8 matrices is symmetric. `atom_center`: in each block of 4 atoms of one owner, at least one atom sits on cell 0 and at least one on cell 1.
All inputs are finite; a program needn't handle non-finite values.
Results may differ from a plain program's by a relative error of at most 0.0027.
Values may be sent and summed in bfloat16 or wider, within the bound.
A program may use at most 32 MiB of HBM per device.

v0:
```python
import jax
import jax.numpy as jnp
from jax import lax
from jax.sharding import PartitionSpec as P

PROJECTORS = 16
STEPS = 3
FACE = 49
CELL_NODES = 343
STRIDE = 294


lower_edge = 4.0
upper_edge = 12.0
ground_edge = -2.0


def with_halo(shard, sides, width):
    for axis, dim in sides:
        peers, length = (lax.axis_size(axis), shard.shape[dim])
        up = [(i, (i + 1) % peers) for i in range(peers)]
        down = [(j, i) for i, j in up]
        last = lax.slice_in_dim(shard, length - width, length, axis=dim)
        initial = lax.slice_in_dim(shard, 0, width, axis=dim)
        before = lax.ppermute(last, axis, up)
        after = lax.ppermute(initial, axis, down)
        shard = jnp.concatenate([before, shard, after], axis=dim)
    return shard


def split_cells(node_block):
    tile_count = (node_block.shape[0] - FACE) // STRIDE
    columns = node_block.shape[1]
    head_rows = node_block[: tile_count * STRIDE].reshape(tile_count, STRIDE, columns)
    padded = jnp.pad(node_block, ((0, STRIDE - FACE), (0, 0)))
    face_rows = padded[STRIDE : STRIDE + tile_count * STRIDE].reshape(tile_count, STRIDE, columns)[
        :, :FACE
    ]
    return jnp.concatenate([head_rows, face_rows], axis=1)


def join_cells(cell_tiles):
    tile_count = cell_tiles.shape[0]
    columns = cell_tiles.shape[2]
    head_rows = cell_tiles[:, :STRIDE].reshape(tile_count * STRIDE, columns)
    tail_rows = jnp.pad(cell_tiles[:, STRIDE:], ((0, 0), (0, STRIDE - FACE), (0, 0))).reshape(
        tile_count * STRIDE, columns
    )
    return (
        jnp.pad(head_rows, ((0, FACE), (0, 0)))
        + jnp.pad(tail_rows, ((STRIDE, 0), (0, 0)))[: tile_count * STRIDE + FACE]
    )


def body(filter_input, cell_table, cell_type, atom_center, proj_values, coupling, occupation):
    cell_count = cell_type.shape[0]
    atom_count = atom_center.shape[0]
    states_local = filter_input.shape[1]
    node_rows = filter_input.shape[0]
    coef_rows = atom_count * PROJECTORS
    matrices = jnp.take(cell_table, cell_type, axis=0)
    picks = atom_center[:, None] + jnp.arange(3, dtype=jnp.int32)[None, :]
    onehot = (
        picks[:, :, None] == jnp.arange(cell_count + 2, dtype=jnp.int32)[None, None, :]
    ).astype(jnp.float32)
    beta_cells = jnp.einsum(
        "ajk,ajpr->kapr", onehot, proj_values.astype(jnp.float32), precision=lax.Precision.HIGHEST
    )
    beta_cells = beta_cells.reshape(cell_count + 2, coef_rows, CELL_NODES).astype(jnp.bfloat16)

    def apply_h(current):
        rounded = current.astype(jnp.bfloat16)
        x_rims = with_halo(rounded[FACE:-FACE], (("cells", 0),), STRIDE)
        extended = jnp.concatenate([x_rims[:STRIDE], rounded, x_rims[-STRIDE:]], axis=0)
        ext_tiles = split_cells(extended)
        cell_terms = jnp.einsum(
            "cij,cjs->cis", matrices, ext_tiles[1:-1], preferred_element_type=jnp.float32
        )
        coeffs = jnp.einsum(
            "kqr,krs->qs", beta_cells, ext_tiles, preferred_element_type=jnp.float32
        )
        weighted = jnp.einsum(
            "pq,aqs->aps",
            coupling,
            coeffs.reshape(atom_count, PROJECTORS, states_local),
            precision=lax.Precision.HIGHEST,
        )
        flat_weighted = weighted.astype(jnp.bfloat16).reshape(coef_rows, states_local)
        spread = jnp.einsum(
            "kqr,qs->krs", beta_cells, flat_weighted, preferred_element_type=jnp.float32
        )
        summed = join_cells(spread + jnp.pad(cell_terms, ((1, 1), (0, 0), (0, 0))))
        outer_rows = with_halo(summed, (("cells", 0),), CELL_NODES)
        mine_rows = summed[STRIDE : STRIDE + node_rows]
        lower_part = jnp.pad(outer_rows[:CELL_NODES], ((0, node_rows - CELL_NODES), (0, 0)))
        upper_part = jnp.pad(outer_rows[-CELL_NODES:], ((node_rows - CELL_NODES, 0), (0, 0)))
        return mine_rows + lower_part + upper_part

    half_width = (upper_edge - lower_edge) / 2.0
    centre = (upper_edge + lower_edge) / 2.0
    scale_now = half_width / (ground_edge - centre)
    twice_inverse = 2.0 / scale_now
    previous = filter_input.astype(jnp.float32)
    current = (apply_h(previous) - centre * previous) * (scale_now / half_width)
    for repeat in range(STEPS - 1):
        scale_next = 1.0 / (twice_inverse - scale_now)
        image = apply_h(current)
        upcoming = (image - centre * current) * (
            2.0 * scale_next / half_width
        ) - scale_now * scale_next * previous
        previous, current = (current, upcoming)
        scale_now = scale_next
    squares = jnp.sum(current * current * occupation[None, :], axis=1) / (
        states_local * lax.axis_size("states")
    )
    density = lax.psum(squares, "states")
    return (current, density)


def solution(mesh):
    in_specs = (
        P("cells", "states"),
        P(),
        P("cells"),
        P("cells"),
        P("cells", None, None, None),
        P(),
        P("states"),
    )
    out_specs = (P("cells", "states"), P("cells"))
    return jax.shard_map(body, mesh=mesh, in_specs=in_specs, out_specs=out_specs, check_vma=False)
```

profile of v0, /device:TPU:2, one launch (start us, length us, event | category | flops | bytes accessed | tf_op | source)
XLA Modules:
  0.0 153.6 jit_solution(7050758074061735051)
XLA Ops:
  0.6 1.1 fusion.70
  1.8 20.5 %collective-permute-start.1 = (bf16[294,128]{1,0:T(8,128)(2,1)S(1)}, bf16[294,128]{1,0:T(8,128)(2,1)S(1)}, u32[]{:S(2)}, u32[]{:S(2)}) collective-permute-start(bf16[294,128]{1,0:T(8,128)(2,1)S(1)} %get-tuple-element.22), channel_id=1, source_target_pairs={{8,0},{16,8},{24,16},{32,24},{40,32},{48,40},{56,48},{64,56},{72,6... | collective-permute-start | bytes 225800 | tf_op jit(solution)/shard_map/ppermute | solution.py:26
  22.2 1.9 %collective-permute-start = (bf16[294,128]{1,0:T(8,128)(2,1)S(1)}, bf16[294,128]{1,0:T(8,128)(2,1)S(1)}, u32[]{:S(2)}, u32[]{:S(2)}) collective-permute-start(bf16[294,128]{1,0:T(8,128)(2,1)S(1)} %get-tuple-element.23), channel_id=1, source_target_pairs={{0,8},{8,16},{16,24},{24,32},{32,40},{40,48},{48,56},{56,64},{64,7... | collective-permute-start | bytes 225800 | tf_op jit(solution)/shard_map/ppermute | solution.py:25
  24.2 0.7 compare_and_fusion
  24.8 0.7 compare_select_fusion
  25.5 0.7 iota_add_fusion
  26.2 4.6 %gather_fusion = bf16[2,343,343]{2,0,1:T(2,128)(2,1)S(1)} fusion(bf16[8,343,343]{2,0,1:T(8,128)(2,1)S(1)} %copy-done, s32[1024]{0:T(1024)S(1)} %pad_clamp_fusion), kind=kCustom, calls=%fused_computation | custom fusion | bytes 941200 | tf_op jit(solution)/shard_map/jit(_take)/gather | solution.py:61
  30.9 1.4 broadcast_select_fusion
  32.3 0.9 convolution_convert_fusion
  33.2 1.0 concatenate.18
  34.3 0.1 fusion.67
  34.5 1.2 convolution_bitcast_fusion.5
  35.7 1.4 fusion.13
  37.1 0.2 fusion.3
  37.3 1.3 fusion
  38.7 0.9 reshape.83
  39.6 0.9 reshape.84
  40.4 1.3 fusion.6
  41.8 1.9 %collective-permute-start.2 = (f32[343,128]{1,0:T(8,128)S(1)}, f32[343,128]{1,0:T(8,128)S(1)}, u32[]{:S(2)}, u32[]{:S(2)}) collective-permute-start(f32[343,128]{1,0:T(8,128)S(1)} %get-tuple-element.10), channel_id=1, source_target_pairs={{0,8},{8,16},{16,24},{24,32},{32,40},{40,48},{48,56},{56,64},{64,7... | collective-permute-start | bytes 526856 | tf_op jit(solution)/shard_map/ppermute | solution.py:25
  43.7 7.0 %collective-permute-start.3 = (f32[343,128]{1,0:T(8,128)S(1)}, f32[343,128]{1,0:T(8,128)S(1)}, u32[]{:S(2)}, u32[]{:S(2)}) collective-permute-start(f32[343,128]{1,0:T(8,128)S(1)} %get-tuple-element.11), channel_id=1, source_target_pairs={{8,0},{16,8},{24,16},{32,24},{40,32},{48,40},{56,48},{64,56},{72,6... | collective-permute-start | bytes 526856 | tf_op jit(solution)/shard_map/ppermute | solution.py:26
  50.7 1.2 collective-permute-done.2
  51.8 1.8 %collective-permute-done.3 = f32[343,128]{1,0:T(8,128)S(1)} collective-permute-done((f32[343,128]{1,0:T(8,128)S(1)}, f32[343,128]{1,0:T(8,128)S(1)}, u32[]{:S(2)}, u32[]{:S(2)}) %collective-permute-start.3) | collective-permute-done | bytes 175648 | tf_op jit(solution)/shard_map/ppermute | solution.py:26
  53.6 0.1 multiply_convert_fusion
  53.8 7.1 %collective-permute-start.5 = (bf16[294,128]{1,0:T(8,128)(2,1)S(1)}, bf16[294,128]{1,0:T(8,128)(2,1)S(1)}, u32[]{:S(2)}, u32[]{:S(2)}) collective-permute-start(bf16[294,128]{1,0:T(8,128)(2,1)S(1)} %get-tuple-element.20), channel_id=1, source_target_pairs={{8,0},{16,8},{24,16},{32,24},{40,32},{48,40},{56,48},{64,56},{72,6... | collective-permute-start | bytes 225800 | tf_op jit(solution)/shard_map/ppermute | solution.py:26
  60.9 1.9 %collective-permute-start.4 = (bf16[294,128]{1,0:T(8,128)(2,1)S(1)}, bf16[294,128]{1,0:T(8,128)(2,1)S(1)}, u32[]{:S(2)}, u32[]{:S(2)}) collective-permute-start(bf16[294,128]{1,0:T(8,128)(2,1)S(1)} %get-tuple-element.21), channel_id=1, source_target_pairs={{0,8},{8,16},{16,24},{24,32},{32,40},{40,48},{48,56},{56,64},{64,7... | collective-permute-start | bytes 225800 | tf_op jit(solution)/shard_map/ppermute | solution.py:25
  62.9 7.0 %collective-permute-done.4 = bf16[294,128]{1,0:T(8,128)(2,1)S(1)} collective-permute-done((bf16[294,128]{1,0:T(8,128)(2,1)S(1)}, bf16[294,128]{1,0:T(8,128)(2,1)S(1)}, u32[]{:S(2)}, u32[]{:S(2)}) %collective-permute-start.4) | collective-permute-done | bytes 75296 | tf_op jit(solution)/shard_map/ppermute | solution.py:25
  69.9 1.0 concatenate.20
  70.9 0.1 fusion.66
  71.0 0.8 reshape.85
  71.9 1.3 convolution_bitcast_fusion.4
  73.2 1.4 fusion.11
  74.6 0.2 fusion.4
  74.8 1.3 fusion.1
  76.2 0.9 reshape.87
  77.1 0.9 reshape.88
  78.0 1.3 fusion.7
  79.3 1.9 %collective-permute-start.6 = (f32[343,128]{1,0:T(8,128)S(1)}, f32[343,128]{1,0:T(8,128)S(1)}, u32[]{:S(2)}, u32[]{:S(2)}) collective-permute-start(f32[343,128]{1,0:T(8,128)S(1)} %get-tuple-element.8), channel_id=1, source_target_pairs={{0,8},{8,16},{16,24},{24,32},{32,40},{40,48},{48,56},{56,64},{64,7... | collective-permute-start | bytes 526856 | tf_op jit(solution)/shard_map/ppermute | solution.py:25
  81.2 7.0 %collective-permute-start.7 = (f32[343,128]{1,0:T(8,128)S(1)}, f32[343,128]{1,0:T(8,128)S(1)}, u32[]{:S(2)}, u32[]{:S(2)}) collective-permute-start(f32[343,128]{1,0:T(8,128)S(1)} %get-tuple-element.9), channel_id=1, source_target_pairs={{8,0},{16,8},{24,16},{32,24},{40,32},{48,40},{56,48},{64,56},{72,6... | collective-permute-start | bytes 526856 | tf_op jit(solution)/shard_map/ppermute | solution.py:26
  88.2 1.2 collective-permute-done.6
  89.4 1.8 %collective-permute-done.7 = f32[343,128]{1,0:T(8,128)S(1)} collective-permute-done((f32[343,128]{1,0:T(8,128)S(1)}, f32[343,128]{1,0:T(8,128)S(1)}, u32[]{:S(2)}, u32[]{:S(2)}) %collective-permute-start.7) | collective-permute-done | bytes 175648 | tf_op jit(solution)/shard_map/ppermute | solution.py:26
  91.1 0.1 fusion.59
  91.3 7.1 %collective-permute-start.9 = (bf16[294,128]{1,0:T(8,128)(2,1)S(1)}, bf16[294,128]{1,0:T(8,128)(2,1)S(1)}, u32[]{:S(2)}, u32[]{:S(2)}) collective-permute-start(bf16[294,128]{1,0:T(8,128)(2,1)S(1)} %get-tuple-element.18), channel_id=1, source_target_pairs={{8,0},{16,8},{24,16},{32,24},{40,32},{48,40},{56,48},{64,56},{72,6... | collective-permute-start | bytes 225800 | tf_op jit(solution)/shard_map/ppermute | solution.py:26
  98.5 1.9 %collective-permute-start.8 = (bf16[294,128]{1,0:T(8,128)(2,1)S(1)}, bf16[294,128]{1,0:T(8,128)(2,1)}, u32[]{:S(2)}, u32[]{:S(2)}) collective-permute-start(bf16[294,128]{1,0:T(8,128)(2,1)S(1)} %get-tuple-element.19), channel_id=1, source_target_pairs={{0,8},{8,16},{16,24},{24,32},{32,40},{40,48},{48,56},{56,64},{64,7... | collective-permute-start | bytes 225800 | tf_op jit(solution)/shard_map/ppermute | solution.py:25
  100.5 0.6 copy-done.7
  101.1 6.5 %collective-permute-done.8 = bf16[294,128]{1,0:T(8,128)(2,1)} collective-permute-done((bf16[294,128]{1,0:T(8,128)(2,1)S(1)}, bf16[294,128]{1,0:T(8,128)(2,1)}, u32[]{:S(2)}, u32[]{:S(2)}) %collective-permute-start.8) | collective-permute-done | bytes 75296 | tf_op jit(solution)/shard_map/ppermute | solution.py:25
  107.6 2.9 %concatenate.22 = bf16[1225,128]{1,0:T(8,128)(2,1)S(1)} concatenate(bf16[294,128]{1,0:T(8,128)(2,1)} %collective-permute-done.8, bf16[637,128]{1,0:T(8,128)(2,1)} %copy-done.2, bf16[294,128]{1,0:T(8,128)(2,1)} %copy-done.7), dimensions={0} | concatenate | bytes 627200 | tf_op jit(solution)/shard_map/concatenate | solution.py:74
  110.5 0.9 fusion.65
  111.4 1.8 %reshape.89 = bf16[4,294,128]{2,1,0:T(8,128)(2,1)} reshape(bf16[1176,128]{1,0:T(8,128)(2,1)} %get-tuple-element.12) | data formatting | bytes 602112 | tf_op jit(solution)/shard_map/reshape | solution.py:34
  113.1 1.0 reshape.90
  114.2 1.4 fusion.9
  115.6 1.3 convolution_bitcast_fusion.3
  116.9 0.2 fusion.5
  117.1 0.4 fusion.2
  117.5 0.9 slice.181
  118.4 1.9 %reshape.91 = f32[1176,128]{1,0:T(8,128)} reshape(f32[4,294,128]{2,1,0:T(8,128)} %slice.181) | data formatting | bytes 1204224 | tf_op jit(solution)/shard_map/reshape | solution.py:45
  120.3 0.9 pad.87
  121.2 1.9 %reshape.92 = f32[1176,128]{1,0:T(8,128)} reshape(f32[4,294,128]{2,1,0:T(8,128)} %pad.87) | data formatting | bytes 1204224 | tf_op jit(solution)/shard_map/reshape | solution.py:46
  123.1 1.3 fusion.8
  124.5 1.9 %collective-permute-start.10 = (f32[343,128]{1,0:T(8,128)S(1)}, f32[343,128]{1,0:T(8,128)S(1)}, u32[]{:S(2)}, u32[]{:S(2)}) collective-permute-start(f32[343,128]{1,0:T(8,128)S(1)} %get-tuple-element.6), channel_id=1, source_target_pairs={{0,8},{8,16},{16,24},{24,32},{32,40},{40,48},{48,56},{56,64},{64,7... | collective-permute-start | bytes 526856 | tf_op jit(solution)/shard_map/ppermute | solution.py:25
  126.4 7.0 %collective-permute-start.11 = (f32[343,128]{1,0:T(8,128)S(1)}, f32[343,128]{1,0:T(8,128)S(1)}, u32[]{:S(2)}, u32[]{:S(2)}) collective-permute-start(f32[343,128]{1,0:T(8,128)S(1)} %get-tuple-element.7), channel_id=1, source_target_pairs={{8,0},{16,8},{24,16},{32,24},{40,32},{48,40},{56,48},{64,56},{72,6... | collective-permute-start | bytes 526856 | tf_op jit(solution)/shard_map/ppermute | solution.py:26
  133.4 1.2 collective-permute-done.10
  134.6 1.8 %collective-permute-done.11 = f32[343,128]{1,0:T(8,128)S(1)} collective-permute-done((f32[343,128]{1,0:T(8,128)S(1)}, f32[343,128]{1,0:T(8,128)S(1)}, u32[]{:S(2)}, u32[]{:S(2)}) %collective-permute-start.11) | collective-permute-done | bytes 175648 | tf_op jit(solution)/shard_map/ppermute | solution.py:26
  136.3 1.0 multiply_reduce_fusion
  137.3 16.3 %psum.7 = f32[637]{0:T(1024)} all-reduce(f32[637]{0:T(1024)S(1)} %broadcast_multiply_fusion), channel_id=1, replica_groups=mesh['cells'=128,'states'=8] {'states'}, use_global_device_ids=true, to_apply=%region_1.2 | all-reduce | flops 637 | bytes 5096 | tf_op jit(solution)/shard_map/psum | solution.py:116
  (47 shorter events, 0.8 us)
Async XLA Ops:
  0.6 25.6 %copy-start = (bf16[8,343,343]{2,0,1:T(8,128)(2,1)S(1)}, bf16[8,343,343]{2,0,1:T(8,128)(2,1)}, u32[]{:S(2)}) copy-start(bf16[8,343,343]{2,0,1:T(8,128)(2,1)} %param.8) | copy-start | bytes 5647156
  1.8 31.5 %collective-permute-start.1 = (bf16[294,128]{1,0:T(8,128)(2,1)S(1)}, bf16[294,128]{1,0:T(8,128)(2,1)S(1)}, u32[]{:S(2)}, u32[]{:S(2)}) collective-permute-start(bf16[294,128]{1,0:T(8,128)(2,1)S(1)} %get-tuple-element.22), channel_id=1, source_target_pairs={{8,0},{16,8},{24,16},{32,24},{40,32},{48,40},{56,48},{64,56},{72,6... | collective-permute-start | bytes 225800 | tf_op jit(solution)/shard_map/ppermute | solution.py:26
  22.2 11.0 %collective-permute-start = (bf16[294,128]{1,0:T(8,128)(2,1)S(1)}, bf16[294,128]{1,0:T(8,128)(2,1)S(1)}, u32[]{:S(2)}, u32[]{:S(2)}) collective-permute-start(bf16[294,128]{1,0:T(8,128)(2,1)S(1)} %get-tuple-element.23), channel_id=1, source_target_pairs={{0,8},{8,16},{16,24},{24,32},{32,40},{40,48},{48,56},{56,64},{64,7... | collective-permute-start | bytes 225800 | tf_op jit(solution)/shard_map/ppermute | solution.py:25
  26.2 6.1 %copy-start.10 = (bf16[4,3,16,343]{3,2,1,0:T(8,128)(2,1)S(1)}, bf16[4,3,16,343]{3,2,1,0:T(8,128)(2,1)}, u32[]{:S(2)}) copy-start(bf16[4,3,16,343]{3,2,1,0:T(8,128)(2,1)} %param.11) | copy-start | bytes 395140
  26.2 7.0 %copy-start.1 = (bf16[637,128]{1,0:T(8,128)(2,1)S(1)}, bf16[637,128]{1,0:T(8,128)(2,1)}, u32[]{:S(2)}) copy-start(bf16[637,128]{1,0:T(8,128)(2,1)} %param.7) | copy-start | bytes 489220
  34.2 2.9 %copy-start.8 = (f32[16,16]{1,0:T(8,128)S(1)}, f32[16,16]{1,0:T(8,128)}, u32[]{:S(2)}) copy-start(f32[16,16]{1,0:T(8,128)} %param.12) | copy-start | bytes 3076
  41.8 10.1 %collective-permute-start.2 = (f32[343,128]{1,0:T(8,128)S(1)}, f32[343,128]{1,0:T(8,128)S(1)}, u32[]{:S(2)}, u32[]{:S(2)}) collective-permute-start(f32[343,128]{1,0:T(8,128)S(1)} %get-tuple-element.10), channel_id=1, source_target_pairs={{0,8},{8,16},{16,24},{24,32},{32,40},{40,48},{48,56},{56,64},{64,7... | collective-permute-start | bytes 526856 | tf_op jit(solution)/shard_map/ppermute | solution.py:25
  43.7 9.9 %collective-permute-start.3 = (f32[343,128]{1,0:T(8,128)S(1)}, f32[343,128]{1,0:T(8,128)S(1)}, u32[]{:S(2)}, u32[]{:S(2)}) collective-permute-start(f32[343,128]{1,0:T(8,128)S(1)} %get-tuple-element.11), channel_id=1, source_target_pairs={{8,0},{16,8},{24,16},{32,24},{40,32},{48,40},{56,48},{64,56},{72,6... | collective-permute-start | bytes 526856 | tf_op jit(solution)/shard_map/ppermute | solution.py:26
  53.8 9.1 %collective-permute-start.5 = (bf16[294,128]{1,0:T(8,128)(2,1)S(1)}, bf16[294,128]{1,0:T(8,128)(2,1)S(1)}, u32[]{:S(2)}, u32[]{:S(2)}) collective-permute-start(bf16[294,128]{1,0:T(8,128)(2,1)S(1)} %get-tuple-element.20), channel_id=1, source_target_pairs={{8,0},{16,8},{24,16},{32,24},{40,32},{48,40},{56,48},{64,56},{72,6... | collective-permute-start | bytes 225800 | tf_op jit(solution)/shard_map/ppermute | solution.py:26
  60.9 9.0 %collective-permute-start.4 = (bf16[294,128]{1,0:T(8,128)(2,1)S(1)}, bf16[294,128]{1,0:T(8,128)(2,1)S(1)}, u32[]{:S(2)}, u32[]{:S(2)}) collective-permute-start(bf16[294,128]{1,0:T(8,128)(2,1)S(1)} %get-tuple-element.21), channel_id=1, source_target_pairs={{0,8},{8,16},{16,24},{24,32},{32,40},{40,48},{48,56},{56,64},{64,7... | collective-permute-start | bytes 225800 | tf_op jit(solution)/shard_map/ppermute | solution.py:25
  79.3 10.1 %collective-permute-start.6 = (f32[343,128]{1,0:T(8,128)S(1)}, f32[343,128]{1,0:T(8,128)S(1)}, u32[]{:S(2)}, u32[]{:S(2)}) collective-permute-start(f32[343,128]{1,0:T(8,128)S(1)} %get-tuple-element.8), channel_id=1, source_target_pairs={{0,8},{8,16},{16,24},{24,32},{32,40},{40,48},{48,56},{56,64},{64,7... | collective-permute-start | bytes 526856 | tf_op jit(solution)/shard_map/ppermute | solution.py:25
  81.2 9.9 %collective-permute-start.7 = (f32[343,128]{1,0:T(8,128)S(1)}, f32[343,128]{1,0:T(8,128)S(1)}, u32[]{:S(2)}, u32[]{:S(2)}) collective-permute-start(f32[343,128]{1,0:T(8,128)S(1)} %get-tuple-element.9), channel_id=1, source_target_pairs={{8,0},{16,8},{24,16},{32,24},{40,32},{48,40},{56,48},{64,56},{72,6... | collective-permute-start | bytes 526856 | tf_op jit(solution)/shard_map/ppermute | solution.py:26
  89.4 11.1 %copy-start.3 = (f32[343,128]{1,0:T(8,128)}, f32[343,128]{1,0:T(8,128)S(1)}, u32[]{:S(2)}) copy-start(f32[343,128]{1,0:T(8,128)S(1)} %collective-permute-done.6) | copy-start | bytes 526852
  91.1 9.3 %copy-start.5 = (f32[343,128]{1,0:T(8,128)}, f32[343,128]{1,0:T(8,128)S(1)}, u32[]{:S(2)}) copy-start(f32[343,128]{1,0:T(8,128)S(1)} %collective-permute-done.7) | copy-start | bytes 526852
  91.3 9.2 %copy-start.2 = (bf16[637,128]{1,0:T(8,128)(2,1)}, bf16[637,128]{1,0:T(8,128)(2,1)S(1)}, u32[]{:S(2)}) copy-start(bf16[637,128]{1,0:T(8,128)(2,1)S(1)} %fusion.59) | copy-start | bytes 489220
  91.3 9.1 %collective-permute-start.9 = (bf16[294,128]{1,0:T(8,128)(2,1)S(1)}, bf16[294,128]{1,0:T(8,128)(2,1)S(1)}, u32[]{:S(2)}, u32[]{:S(2)}) collective-permute-start(bf16[294,128]{1,0:T(8,128)(2,1)S(1)} %get-tuple-element.18), channel_id=1, source_target_pairs={{8,0},{16,8},{24,16},{32,24},{40,32},{48,40},{56,48},{64,56},{72,6... | collective-permute-start | bytes 225800 | tf_op jit(solution)/shard_map/ppermute | solution.py:26
  98.5 9.1 %collective-permute-start.8 = (bf16[294,128]{1,0:T(8,128)(2,1)S(1)}, bf16[294,128]{1,0:T(8,128)(2,1)}, u32[]{:S(2)}, u32[]{:S(2)}) collective-permute-start(bf16[294,128]{1,0:T(8,128)(2,1)S(1)} %get-tuple-element.19), channel_id=1, source_target_pairs={{0,8},{8,16},{16,24},{24,32},{32,40},{40,48},{48,56},{56,64},{64,7... | collective-permute-start | bytes 225800 | tf_op jit(solution)/shard_map/ppermute | solution.py:25
  100.5 0.6 copy-start.7
  114.2 3.0 %copy-start.11 = (bf16[4,4,16,343]{3,1,2,0:T(4,128)(2,1)S(1)}, bf16[4,4,16,343]{3,1,2,0:T(4,128)(2,1)}, u32[]{:S(2)}) copy-start(bf16[4,4,16,343]{3,1,2,0:T(4,128)(2,1)} %convolution_convert_fusion) | copy-start | bytes 526852
  120.3 16.0 %copy-start.4 = (f32[343,128]{1,0:T(8,128)S(1)}, f32[343,128]{1,0:T(8,128)}, u32[]{:S(2)}) copy-start(f32[343,128]{1,0:T(8,128)} %copy-done.3) | copy-start | bytes 526852
  120.3 16.0 %copy-start.9 = (f32[128]{0:T(128)S(1)}, f32[128]{0:T(128)}, u32[]{:S(2)}) copy-start(f32[128]{0:T(128)} %param.13) | copy-start | bytes 1540
  123.1 13.2 %copy-start.6 = (f32[343,128]{1,0:T(8,128)S(1)}, f32[343,128]{1,0:T(8,128)}, u32[]{:S(2)}) copy-start(f32[343,128]{1,0:T(8,128)} %copy-done.5) | copy-start | bytes 526852
  124.5 10.1 %collective-permute-start.10 = (f32[343,128]{1,0:T(8,128)S(1)}, f32[343,128]{1,0:T(8,128)S(1)}, u32[]{:S(2)}, u32[]{:S(2)}) collective-permute-start(f32[343,128]{1,0:T(8,128)S(1)} %get-tuple-element.6), channel_id=1, source_target_pairs={{0,8},{8,16},{16,24},{24,32},{32,40},{40,48},{48,56},{56,64},{64,7... | collective-permute-start | bytes 526856 | tf_op jit(solution)/shard_map/ppermute | solution.py:25
  126.4 9.9 %collective-permute-start.11 = (f32[343,128]{1,0:T(8,128)S(1)}, f32[343,128]{1,0:T(8,128)S(1)}, u32[]{:S(2)}, u32[]{:S(2)}) collective-permute-start(f32[343,128]{1,0:T(8,128)S(1)} %get-tuple-element.7), channel_id=1, source_target_pairs={{8,0},{16,8},{24,16},{32,24},{40,32},{48,40},{56,48},{64,56},{72,6... | collective-permute-start | bytes 526856 | tf_op jit(solution)/shard_map/ppermute | solution.py:26
where the time goes:
time: 155 us; the launch traced here: 154 us
  starting transfers between devices  67.1 us (43%)
  local copies, waits for them, and re-layouts  25.7 us (17%)
  waiting for transfers between devices  22.5 us (15%)
  blocking collectives  16.3 us (11%)
  matrix products  12.4 us (8%)
  other arithmetic  8.52 us (5%)
    ppermute x6, starting transfers between devices, with_halo(): after = lax.ppermute(initial, axis, down)  55.6 us
    ppermute x6, waiting for transfers between devices, with_halo(): before = lax.ppermute(last, axis, up)  17.1 us
    psum x1, blocking collectives, body(): density = lax.psum(squares, 'states')  16.3 us
    ppermute x6, starting transfers between devices, with_halo(): before = lax.ppermute(last, axis, up)  11.5 us
    ppermute x6, waiting for transfers between devices, with_halo(): after = lax.ppermute(initial, axis, down)  5.37 us
    concatenate x3, local copies, waits for them, and re-layouts, apply_h(): jnp.concatenate([x_rims[:STRIDE], rounded, x_rims[-STRIDE:]], axis=0)  4.85 us
    gather x1, local copies, waits for them, and re-layouts, body(): matrices = jnp.take(cell_table, cell_type, axis=0)  4.65 us
    dot_general x3, matrix products, apply_h(): jnp.einsum('cij,cjs->cis', matrices, ext_tiles[1:-1], preferred_element_t...  4.23 us
  transfers between devices with their start and end apart: 12, of which 10 were waited for; matrix products, arithmetic and copies ran while one was open for 6% of the time, Pallas kernels for 0%

commit v1 on v0

v1 whole, which is shorter than its diff:
```python
import functools

import jax
import jax.numpy as jnp
from jax import lax
from jax.experimental import pallas as pl
from jax.experimental.pallas import tpu as pltpu
from jax.sharding import PartitionSpec as P

PROJECTORS = 16
STEPS = 3
FACE = 49
CELL_NODES = 343
STRIDE = 294
CELL_DEV = 2
NTYPE = 8
ATOM_DEV = 4
NODE_DEV = 637
STATE_DEV = 128
COEFS = ATOM_DEV * PROJECTORS

lower_edge = 4.0
upper_edge = 12.0
ground_edge = -2.0

DEPTH = 384
ROWS = 352
FIELD = 688
TAIL = 288
TAIL_SKIP = STRIDE - TAIL
TAIL_COL = 256
FACE_PAD = 56

BF = jnp.bfloat16
F32 = jnp.float32
LINK = jnp.float32
MESH = pl.DeviceIdType.MESH


def mm(a, b):
    return jnp.dot(a, b, preferred_element_type=F32)


def mm_nt(a, b):
    return lax.dot_general(a, b, (((1,), (1,)), ((), ())), preferred_element_type=F32)


def scales():
    half_width = (upper_edge - lower_edge) / 2.0
    scale_now = half_width / (ground_edge - (upper_edge + lower_edge) / 2.0)
    twice_inverse = 2.0 / scale_now
    pairs = [(scale_now / half_width, 0.0)]
    for _ in range(STEPS - 1):
        scale_next = 1.0 / (twice_inverse - scale_now)
        pairs.append((2.0 * scale_next / half_width, scale_now * scale_next))
        scale_now = scale_next
    return pairs


def kernel(
    nc,
    ns,
    x_hbm,
    tab_hbm,
    type_ref,
    center_ref,
    proj_hbm,
    coup_ref,
    occ_ref,
    out_x,
    out_d,
    xin,
    tab,
    proj,
    hwide,
    hmat,
    own,
    ends_send,
    ends_recv,
    spread_mat,
    face_wide,
    face_mat,
    mix,
    field,
    last,
    own_send,
    own_recv,
    side_send,
    side_recv,
    dens_send,
    dens_recv,
    load_sem,
    ends_sems,
    own_sems,
    near_sems,
    far_sems,
    dens_sems,
):
    here = lax.axis_index("cells")
    column = lax.axis_index("states")

    def cell_at(shift):
        return {"cells": lax.rem(here + (shift + nc), nc)}

    def state_at(shift):
        return {"states": lax.rem(column + shift, ns)}

    barrier = pltpu.get_barrier_semaphore()
    for shift in (-2, -1, 1, 2):
        pl.semaphore_signal(barrier, inc=1, device_id=cell_at(shift), device_id_type=MESH)
    for shift in range(1, ns):
        pl.semaphore_signal(barrier, inc=1, device_id=state_at(shift), device_id_type=MESH)

    loads = [
        pltpu.make_async_copy(proj_hbm, proj, load_sem.at[0]),
        pltpu.make_async_copy(x_hbm, xin, load_sem.at[1]),
        pltpu.make_async_copy(tab_hbm, tab, load_sem.at[2]),
    ]
    for load in loads:
        load.start()

    own[...] = jnp.zeros_like(own)
    dens_send[...] = jnp.zeros_like(dens_send)
    ends_send[...] = jnp.zeros_like(ends_send)
    field[:, NODE_DEV - 5 :, :] = jnp.zeros((STEPS, FIELD - NODE_DEV + 5, STATE_DEV), F32)
    hwide[...] = jnp.zeros_like(hwide)

    loads[0].wait()
    for atom in range(ATOM_DEV):
        first = center_ref[atom] == 0
        rows = pl.ds(atom * PROJECTORS, PROJECTORS)
        before, middle, after = (proj[atom, j].astype(F32) for j in range(3))
        zero = jnp.zeros_like(before)
        on_first = jnp.where(first, middle, before).astype(BF)
        on_second = jnp.where(first, after, middle).astype(BF)
        own[0, rows, :CELL_NODES] = on_first
        own[1, rows, :CELL_NODES] = on_second
        ends_send[0, rows, :CELL_NODES] = jnp.where(first, before, zero).astype(BF)
        ends_send[1, rows, :CELL_NODES] = jnp.where(first, zero, after).astype(BF)
    ends_send[0, :, DEPTH:] = own[0, :, :128]
    ends_send[1, :, DEPTH:] = own[1, :, TAIL_COL:]

    coup = coup_ref[...]
    high = coup.astype(BF)
    low = (coup - high.astype(F32)).astype(BF)
    many = 3 * COEFS
    pick = (
        lax.rem(lax.broadcasted_iota(jnp.int32, (many, PROJECTORS), 0), PROJECTORS)
        == lax.broadcasted_iota(jnp.int32, (many, PROJECTORS), 1)
    )
    pick = jnp.where(pick, 1.0, 0.0).astype(BF)
    same = lax.div(lax.broadcasted_iota(jnp.int32, (many, many), 0), PROJECTORS) == lax.div(
        lax.broadcasted_iota(jnp.int32, (many, many), 1), PROJECTORS
    )
    for index, piece in enumerate((high, low)):
        wide = mm_nt(mm(pick, piece).astype(BF), pick)
        mix[index] = jnp.where(same, wide, 0.0).astype(BF)

    pl.semaphore_wait(barrier, 4 + ns - 1)

    def send(src, dst, sems, slot, device):
        copy = pltpu.make_async_remote_copy(
            src_ref=src,
            dst_ref=dst,
            send_sem=sems.at[0, slot],
            recv_sem=sems.at[1, slot],
            device_id=device,
            device_id_type=MESH,
        )
        copy.start()
        return copy

    ends = [
        send(ends_send.at[0], ends_recv.at[1], ends_sems, 0, cell_at(-1)),
        send(ends_send.at[1], ends_recv.at[0], ends_sems, 1, cell_at(1)),
    ]

    loads[1].wait()
    field[0, :NODE_DEV, :] = xin[...].astype(F32)

    loads[2].wait()
    chunk = 256 // NTYPE
    spot = lax.broadcasted_iota(jnp.int32, (CELL_DEV * chunk, 256), 0)
    kind = jnp.where(spot < chunk, type_ref[0], type_ref[1])
    take = lax.broadcasted_iota(jnp.int32, (CELL_DEV * chunk, 256), 1) == lax.rem(spot, chunk) * NTYPE + kind
    take = jnp.where(take, 1.0, 0.0).astype(BF)
    for start in range(0, CELL_NODES, chunk):
        count = min(chunk, CELL_NODES - start)
        entries = tab[start : start + count].reshape(count * NTYPE, CELL_NODES)
        rows = mm(take[:, : count * NTYPE], entries)
        for cell in range(CELL_DEV):
            hwide[cell, start : start + count, :CELL_NODES] = rows[cell * chunk : cell * chunk + count]
    hmat[...] = hwide[...].astype(BF)

    pending = []
    for step, (gain, back) in enumerate(scales()):
        x = field.at[step]
        first_cell = x[:DEPTH, :].astype(BF)
        second_cell = x[STRIDE : STRIDE + DEPTH, :].astype(BF)

        mine = mm(own[0], first_cell) + mm(own[1], second_cell)
        face_first = mm(hmat[0, :64, :], first_cell)
        face_second = mm(hmat[1, TAIL : TAIL + 64, :], second_cell)
        own_send[step, 0, :COEFS, :] = mine.astype(LINK)
        own_send[step, 1, :COEFS, :] = mine.astype(LINK)
        own_send[step, 0, COEFS:, :] = face_first[:FACE_PAD].astype(LINK)
        own_send[step, 1, COEFS:, :] = face_second[:FACE_PAD].astype(LINK)
        own_copies = [
            send(own_send.at[step, 0], own_recv.at[step, 1], own_sems.at[step], 0, cell_at(-1)),
            send(own_send.at[step, 1], own_recv.at[step, 0], own_sems.at[step], 1, cell_at(1)),
        ]

        if step == 0:
            for copy in ends:
                copy.wait_recv()
        before = mm(ends_recv[0, :, :DEPTH], first_cell)
        after = mm(ends_recv[1, :, :DEPTH], second_cell)
        side_send[step, 0] = before.astype(LINK)
        side_send[step, 1] = after.astype(LINK)
        far_copies = [
            send(side_send.at[step, 0], side_recv.at[step, 1, 1], far_sems.at[step], 0, cell_at(-2)),
            send(side_send.at[step, 1], side_recv.at[step, 0, 1], far_sems.at[step], 1, cell_at(2)),
        ]
        near_copies = [
            send(side_send.at[step, 0], side_recv.at[step, 1, 0], near_sems.at[step], 0, cell_at(-1)),
            send(side_send.at[step, 1], side_recv.at[step, 0, 0], near_sems.at[step], 1, cell_at(1)),
        ]
        copies = own_copies + far_copies + near_copies
        pending += copies

        target = last if step == STEPS - 1 else field.at[step + 1]
        centre = (upper_edge + lower_edge) / 2.0
        base = (-centre * gain) * x[:NODE_DEV, :]
        if step:
            base = base - back * field[step - 1, :NODE_DEV, :]
        target[:NODE_DEV, :] = base
        target[:CELL_NODES, :] += gain * mm(hmat[0], first_cell)[:CELL_NODES]
        target[STRIDE:NODE_DEV, :] += gain * mm(hmat[1], second_cell)[:CELL_NODES]

        if step == 0:
            spread_mat[0] = jnp.concatenate([ends_recv[0, :, :DEPTH], own[0]], axis=0).astype(F32).T.astype(BF)
            spread_mat[1] = jnp.concatenate([own[1], ends_recv[1, :, :DEPTH]], axis=0).astype(F32).T.astype(BF)
            face_wide[0] = jnp.concatenate(
                [ends_recv[0, :, DEPTH:], ends_send[0, :, TAIL_COL:DEPTH]], axis=0
            ).astype(F32).T
            face_wide[1] = jnp.concatenate(
                [ends_send[1, :, :128], ends_recv[1, :, DEPTH:]], axis=0
            ).astype(F32).T
            skip = STRIDE - TAIL_COL
            face_mat[0] = face_wide[0, skip : skip + FACE_PAD, :].astype(BF)
            face_mat[1] = face_wide[1, :FACE_PAD, :].astype(BF)

        for copy in copies:
            copy.wait_recv()
        got = own_recv[step].astype(F32)
        sides = side_recv[step].astype(F32)
        coeffs = jnp.concatenate(
            [
                before + got[0, :COEFS] + sides[0, 1],
                mine + sides[0, 0] + sides[1, 0],
                after + got[1, :COEFS] + sides[1, 1],
            ],
            axis=0,
        )
        high = coeffs.astype(BF)
        low = (coeffs - high.astype(F32)).astype(BF)
        weighted = (mm(mix[0], high) + mm(mix[1], high) + mm(mix[0], low)).astype(BF)
        left, right = weighted[: 2 * COEFS], weighted[COEFS:]
        target[:CELL_NODES, :] += gain * mm(spread_mat[0], left)[:CELL_NODES]
        target[STRIDE:NODE_DEV, :] += gain * mm(spread_mat[1], right)[:CELL_NODES]
        skip = COEFS + TAIL_SKIP
        target[:FACE, :] += gain * (
            mm(face_mat[0], left)[:FACE] + own_recv[step, 0, skip : skip + FACE, :].astype(F32)
        )
        target[NODE_DEV - FACE : NODE_DEV, :] += gain * (
            mm(face_mat[1], right)[:FACE] + own_recv[step, 1, COEFS : COEFS + FACE, :].astype(F32)
        )

    store = pltpu.make_async_copy(last, out_x, load_sem.at[0])
    store.start()

    square = last[...] * last[...]
    high = square.astype(BF)
    low = (square - high.astype(F32)).astype(BF)
    weight = occ_ref[...] * (1.0 / (STATE_DEV * ns))
    weight_high = weight.astype(BF).astype(F32)
    row = lax.broadcasted_iota(jnp.int32, (16, STATE_DEV), 0)
    weights = jnp.where(row == 0, weight_high, jnp.where(row == 1, weight - weight_high, 0.0)).astype(BF)
    sums = mm_nt(weights, high) + mm_nt(weights, low)
    sums = sums[0:1] + sums[1:2]
    tiles = dens_send.shape[0]
    for tile in range(tiles):
        end = min(NODE_DEV, (tile + 1) * 128)
        dens_send[tile : tile + 1, : end - tile * 128] = sums[:, tile * 128 : end]
    dens_recv[column] = dens_send[...]
    dens_copies = []
    for shift in sorted(range(1, ns), key=lambda k: -min(k, ns - k)):
        dens_copies.append(send(dens_send, dens_recv.at[column], dens_sems, shift - 1, state_at(shift)))
    for copy in dens_copies:
        copy.wait_recv()
    total = dens_recv[0]
    for peer in range(1, ns):
        total = total + dens_recv[peer]
    for tile in range(tiles):
        end = min(NODE_DEV, (tile + 1) * 128)
        out_d[tile * 128 : end] = total[tile, : end - tile * 128]

    for copy in ends + pending + dens_copies:
        copy.wait_send()
    store.wait()


def solution(mesh):
    nc, ns = mesh.shape["cells"], mesh.shape["states"]

    def body(filter_input, cell_table, cell_type, atom_center, proj_values, coupling, occupation):
        any_space = pl.BlockSpec(memory_space=pl.ANY)
        vmem = pl.BlockSpec(memory_space=pltpu.VMEM)
        smem = pl.BlockSpec(memory_space=pltpu.SMEM)
        dma = pltpu.SemaphoreType.DMA
        filtered, density = pl.pallas_call(
            functools.partial(kernel, nc, ns),
            out_shape=(
                jax.ShapeDtypeStruct((NODE_DEV, STATE_DEV), F32),
                jax.ShapeDtypeStruct((NODE_DEV,), F32),
            ),
            in_specs=[any_space, any_space, smem, smem, any_space, vmem, vmem],
            out_specs=(any_space, vmem),
            scratch_shapes=[
                pltpu.VMEM((NODE_DEV, STATE_DEV), BF),
                pltpu.VMEM((CELL_NODES, NTYPE, CELL_NODES), BF),
                pltpu.VMEM(proj_values.shape, BF),
                pltpu.VMEM((CELL_DEV, ROWS, DEPTH), F32),
                pltpu.VMEM((CELL_DEV, ROWS, DEPTH), BF),
                pltpu.VMEM((CELL_DEV, COEFS, DEPTH), BF),
                pltpu.VMEM((2, COEFS, DEPTH + 128), BF),
                pltpu.VMEM((2, COEFS, DEPTH + 128), BF),
                pltpu.VMEM((2, DEPTH, 2 * COEFS), BF),
                pltpu.VMEM((2, 128, 2 * COEFS), F32),
                pltpu.VMEM((2, FACE_PAD, 2 * COEFS), BF),
                pltpu.VMEM((2, 3 * COEFS, 3 * COEFS), BF),
                pltpu.VMEM((STEPS, FIELD, STATE_DEV), F32),
                pltpu.VMEM((NODE_DEV, STATE_DEV), F32),
                pltpu.VMEM((STEPS, 2, COEFS + FACE_PAD, STATE_DEV), LINK),
                pltpu.VMEM((STEPS, 2, COEFS + FACE_PAD, STATE_DEV), LINK),
                pltpu.VMEM((STEPS, 2, COEFS, STATE_DEV), LINK),
                pltpu.VMEM((STEPS, 2, 2, COEFS, STATE_DEV), LINK),
                pltpu.VMEM((5, 128), F32),
                pltpu.VMEM((ns, 5, 128), F32),
                dma((3,)),
                dma((2, 2)),
                dma((STEPS, 2, 2)),
                dma((STEPS, 2, 2)),
                dma((STEPS, 2, 2)),
                dma((2, ns - 1)),
            ],
            compiler_params=pltpu.CompilerParams(collective_id=0, has_side_effects=True),
        )(
            filter_input,
            jnp.swapaxes(cell_table, 0, 1),
            cell_type,
            atom_center,
            proj_values,
            coupling,
            occupation.reshape(1, STATE_DEV),
        )
        return filtered, density

    in_specs = (
        P("cells", "states"),
        P(),
        P("cells"),
        P("cells"),
        P("cells", None, None, None),
        P(),
        P("states"),
    )
    out_specs = (P("cells", "states"), P("cells"))
    return jax.shard_map(body, mesh=mesh, in_specs=in_specs, out_specs=out_specs, check_vma=False)
```

time: 155 us -> 54.5 us (0.35)
  the two profiles are of different devices: /device:TPU:2 before, /device:TPU:1 now
where the time goes in v1:
time: 54.5 us; the launch traced here: 54.3 us
  Pallas kernels  50.6 us (93%)
  local copies, waits for them, and re-layouts  2.99 us (5%)
  between operations  0.64 us (1%)
    pallas_call x1, Pallas kernels, body(): pl.pallas_call(functools.partial(kernel, nc, ns), out_shape=(jax.ShapeDty...  50.6 us
    unnamed x2, local copies, waits for them, and re-layouts  2.99 us

profile of v1, /device:TPU:1, one launch (start us, length us, event | category | flops | bytes accessed | tf_op | source)
XLA Modules:
  0.0 54.3 jit_solution(1671167107011517322)
XLA Ops:
  0.6 50.6 %shard_map.86 = (f32[637,128]{1,0:T(8,128)}, f32[637]{0:T(1024)}) custom-call(bf16[637,128]{1,0:T(8,128)(2,1)} %x_hbm.1, bf16[343,8,343]{2,1,0:T(8,128)(2,1)} %bitcast.2, s32[2]{0:T(128)} %type_ref.1, s32[4]{0:T(128)} %center_ref.1, bf16[4,3,16,343]{3,2,1,0:T(8,128)(2,1)} %proj_hbm.1, f32[16,16]{1,0:T(8,128)} %coup_ref.1, f32[1,128]{1,0:T(1,128)} %bitcast.3), custom_call_target="tpu_custom_call" | custom-call | tf_op jit(solution)/shard_map/pallas_call | solution.py:321
  51.3 1.7 %copy.11 = f32[637,128]{1,0:T(8,128)} copy(f32[637,128]{1,0:T(8,128)} %get-tuple-element.4) | data formatting | bytes 652288
  53.0 1.3 %copy.12 = f32[637]{0:T(1024)} copy(f32[637]{0:T(1024)} %get-tuple-element.5) | data formatting | bytes 5096

commit v2 on v1

v2 whole, which is shorter than its diff:
```python
import functools

import jax
import jax.numpy as jnp
from jax import lax
from jax.experimental import pallas as pl
from jax.experimental.pallas import tpu as pltpu
from jax.sharding import PartitionSpec as P

PROJECTORS = 16
STEPS = 3
FACE = 49
CELL_NODES = 343
STRIDE = 294
CELL_DEV = 2
NTYPE = 8
ATOM_DEV = 4
NODE_DEV = 637
STATE_DEV = 128
COEFS = ATOM_DEV * PROJECTORS

lower_edge = 4.0
upper_edge = 12.0
ground_edge = -2.0

DEPTH = 384
ROWS = 352
WIDE_ROWS = 360
FIELD = 688
TAIL = 288
TAIL_SKIP = STRIDE - TAIL
HEAD_ROWS = 344
TAIL_COL = 256
FACE_PAD = 56
SIDE = COEFS - PROJECTORS
NEAR_ROWS = COEFS + FACE_PAD + SIDE

BF = jnp.bfloat16
F32 = jnp.float32
MESH = pl.DeviceIdType.MESH


def mm(a, b):
    return jnp.dot(a, b, preferred_element_type=F32)


def mm_nt(a, b):
    return lax.dot_general(a, b, (((1,), (1,)), ((), ())), preferred_element_type=F32)


def scales():
    half_width = (upper_edge - lower_edge) / 2.0
    scale_now = half_width / (ground_edge - (upper_edge + lower_edge) / 2.0)
    twice_inverse = 2.0 / scale_now
    pairs = [(scale_now / half_width, 0.0)]
    for _ in range(STEPS - 1):
        scale_next = 1.0 / (twice_inverse - scale_now)
        pairs.append((2.0 * scale_next / half_width, scale_now * scale_next))
        scale_now = scale_next
    return pairs


def split(value):
    high = value.astype(BF)
    return high, (value - high.astype(F32)).astype(BF)


def kernel(
    nc,
    ns,
    x_hbm,
    tab_hbm,
    type_hbm,
    center_hbm,
    proj_hbm,
    coup_hbm,
    occ_hbm,
    out_x,
    out_d,
    xin,
    x_left,
    x_right,
    tab,
    types,
    centers,
    proj,
    coup_ref,
    occ_ref,
    hwide,
    hmat,
    hface,
    own,
    own_mixed,
    edge_mixed,
    side_mixed,
    ends_send,
    ends_recv,
    spread_mat,
    face_wide,
    face_mat,
    field,
    near_send,
    near_recv,
    far_recv,
    whole_send,
    whole_recv,
    dens_send,
    dens_recv,
    load_sem,
    raw_sems,
    ends_sems,
    near_sems,
    whole_sems,
    far_sems,
    dens_sems,
    token_sems,
):
    here = lax.axis_index("cells")
    column = lax.axis_index("states")

    def cell_at(shift):
        return {"cells": lax.rem(here + (shift + nc), nc)}

    def state_at(shift):
        return {"states": lax.rem(column + (shift + ns), ns)}

    barrier = pltpu.get_barrier_semaphore()
    for shift in (-1, 1):
        pl.semaphore_signal(barrier, inc=1, device_id=cell_at(shift), device_id_type=MESH)
        pl.semaphore_signal(barrier, inc=1, device_id=state_at(shift), device_id_type=MESH)

    sources = (center_hbm, proj_hbm, x_hbm, coup_hbm, type_hbm, tab_hbm, occ_hbm)
    targets = (centers, proj, xin, coup_ref, types, tab, occ_ref)
    loads = [pltpu.make_async_copy(*pair, load_sem.at[i]) for i, pair in enumerate(zip(sources, targets))]
    for load in loads:
        load.start()

    def send(src, dst, sems, slot, device):
        copy = pltpu.make_async_remote_copy(
            src_ref=src,
            dst_ref=dst,
            send_sem=sems.at[0, slot],
            recv_sem=sems.at[1, slot],
            device_id=device,
            device_id_type=MESH,
        )
        copy.start()
        return copy

    pl.semaphore_wait(barrier, 4)
    raw = [
        send(x_hbm.at[pl.ds(0, HEAD_ROWS)], x_right, raw_sems, 0, cell_at(-1)),
        send(x_hbm.at[pl.ds(TAIL, NODE_DEV - TAIL)], x_left, raw_sems, 1, cell_at(1)),
    ]

    def tell(turn):
        for shift in (-1 - turn, 1 + turn):
            pl.semaphore_signal(token_sems.at[turn], inc=1, device_id=state_at(shift), device_id_type=MESH)

    turns = 2 if ns > 5 else (1 if ns > 3 else 0)
    if turns > 0:
        tell(0)

    own[...] = jnp.zeros_like(own)
    ends_send[...] = jnp.zeros_like(ends_send)

    loads[0].wait()
    loads[1].wait()
    spots = [centers[atom] for atom in range(ATOM_DEV)]
    on_last = sum(spots)
    on_first = ATOM_DEV - on_last
    places = []
    for atom in range(ATOM_DEV):
        ones = sum(spots[:atom]) if atom else 0
        places.append(jnp.where(spots[atom] == 0, atom - ones, on_first + ones))
    for rank in range(ATOM_DEV):
        atom = sum(jnp.where(places[k] == rank, k, 0) for k in range(ATOM_DEV))
        first = rank < on_first
        rows = pl.ds(rank * PROJECTORS, PROJECTORS)
        before, middle, after = (proj[atom, j].astype(F32) for j in range(3))
        zero = jnp.zeros_like(before)
        own[0, rows, :CELL_NODES] = jnp.where(first, middle, before).astype(BF)
        own[1, rows, :CELL_NODES] = jnp.where(first, after, middle).astype(BF)
        if rank < ATOM_DEV - 1:
            ends_send[0, rows, :CELL_NODES] = jnp.where(first, before, zero).astype(BF)
        if rank > 0:
            ends_send[1, rows, :CELL_NODES] = jnp.where(first, zero, after).astype(BF)
    ends_send[0, :, DEPTH:] = own[0, :, :128]
    ends_send[1, :, DEPTH:] = own[1, :, TAIL_COL:]
    ends = [
        send(ends_send.at[0], ends_recv.at[1], ends_sems, 0, cell_at(-1)),
        send(ends_send.at[1], ends_recv.at[0], ends_sems, 1, cell_at(1)),
    ]

    field[:, NODE_DEV - 5 :, :] = jnp.zeros((STEPS, FIELD - NODE_DEV + 5, STATE_DEV), F32)
    hwide[...] = jnp.zeros_like(hwide)
    dens_send[...] = jnp.zeros_like(dens_send)
    loads[2].wait()
    field[0, :NODE_DEV, :] = xin[...].astype(F32)

    loads[3].wait()
    pick = (
        lax.rem(lax.broadcasted_iota(jnp.int32, (COEFS, PROJECTORS), 0), PROJECTORS)
        == lax.broadcasted_iota(jnp.int32, (COEFS, PROJECTORS), 1)
    )
    pick = jnp.where(pick, 1.0, 0.0).astype(BF)
    same = lax.div(lax.broadcasted_iota(jnp.int32, (COEFS, COEFS), 0), PROJECTORS) == lax.div(
        lax.broadcasted_iota(jnp.int32, (COEFS, COEFS), 1), PROJECTORS
    )
    mix_high, mix_low = (
        jnp.where(same, mm_nt(mm(pick, piece).astype(BF), pick), 0.0).astype(BF) for piece in split(coup_ref[...])
    )

    def mixed(rows):
        return mm(mix_high, rows) + mm(mix_low, rows)

    def fold(both):
        half = both.shape[0] // 2
        return both[:half] + both[half:]

    for cell in range(CELL_DEV):
        own_mixed[cell, :COEFS], own_mixed[cell, COEFS:] = split(mixed(own[cell]))
    turned = pltpu.roll(mixed(ends_send[0, :, :DEPTH]), TAIL_SKIP, 1)
    edge_mixed[0, :COEFS], edge_mixed[0, COEFS:] = split(turned)
    edge_mixed[1, :COEFS], edge_mixed[1, COEFS:] = split(mixed(ends_send[1, :, :DEPTH]))

    loads[4].wait()
    loads[5].wait()
    chunk = 256 // NTYPE
    spot = lax.broadcasted_iota(jnp.int32, (CELL_DEV * chunk, 256), 0)
    kind = jnp.where(spot < chunk, types[0], types[1])
    take = lax.broadcasted_iota(jnp.int32, (CELL_DEV * chunk, 256), 1) == lax.rem(spot, chunk) * NTYPE + kind
    take = jnp.where(take, 1.0, 0.0).astype(BF)
    for start in range(0, CELL_NODES, chunk):
        count = min(chunk, CELL_NODES - start)
        entries = tab[start : start + count].reshape(count * NTYPE, CELL_NODES)
        rows = mm(take[:, : count * NTYPE], entries)
        for cell in range(CELL_DEV):
            hwide[cell, start : start + count, :CELL_NODES] = rows[cell * chunk : cell * chunk + count]
    hmat[...] = hwide[:, :ROWS].astype(BF)
    hface[0] = hwide[0, :COEFS].astype(BF)
    hface[1] = hwide[1, STRIDE : STRIDE + COEFS].astype(BF)

    own_part = slice(0, COEFS)
    face_part = slice(COEFS, COEFS + FACE_PAD)
    side_part = slice(COEFS + FACE_PAD, NEAR_ROWS)
    blank = jnp.zeros((PROJECTORS, STATE_DEV), F32)

    def padded(side, slot):
        return jnp.concatenate([side, blank] if slot else [blank, side], axis=0)

    pending = []
    for step, (gain, back) in enumerate(scales()):
        x = field.at[step]
        cells = (x[:DEPTH, :].astype(BF), x[STRIDE : STRIDE + DEPTH, :].astype(BF))

        mine = fold(mm(own_mixed[0], cells[0]) + mm(own_mixed[1], cells[1]))
        copies = []
        sides = []
        for slot, shift in ((0, -1), (1, 1)):
            near_send[step, slot, face_part] = mm(hface[slot], cells[slot])[:FACE_PAD]
            part = face_part
            if step:
                near_send[step, slot, own_part] = mine
                side = fold(mm(side_mixed[slot], cells[slot]))
                near_send[step, slot, side_part] = side
                sides.append(padded(side, slot))
                part = slice(0, NEAR_ROWS)
            rows = pl.ds(part.start, part.stop - part.start)
            copies.append(
                send(
                    near_send.at[step, slot, rows],
                    near_recv.at[step, 1 - slot, rows],
                    near_sems.at[step],
                    slot,
                    cell_at(shift),
                )
            )
            if step:
                copies.append(
                    send(
                        near_send.at[step, slot, pl.ds(side_part.start, SIDE)],
                        far_recv.at[step - 1, 1 - slot],
                        far_sems.at[step - 1],
                        slot,
                        cell_at(2 * shift),
                    )
                )

        if step == 0:
            for copy in raw:
                copy.wait_recv()
            edges = mm(edge_mixed[0, :, : NODE_DEV - TAIL], x_left[...])
            edges = edges + mm(edge_mixed[1, :, :HEAD_ROWS], x_right[...])
            weighted = (mine + fold(edges)).astype(BF)
            whole_send[...] = weighted
            copies += [
                send(whole_send, whole_recv.at[1 - slot], whole_sems, slot, cell_at(shift))
                for slot, shift in ((0, -1), (1, 1))
            ]
        pending += copies

        target = out_x if step == STEPS - 1 else field.at[step + 1]
        centre = (upper_edge + lower_edge) / 2.0
        base = (-centre * gain) * x[:NODE_DEV, :]
        if step:
            base = base - back * field[step - 1, :NODE_DEV, :]
        target[:NODE_DEV, :] = base
        target[:CELL_NODES, :] += gain * mm(hmat[0], cells[0])[:CELL_NODES]
        target[STRIDE:NODE_DEV, :] += gain * mm(hmat[1], cells[1])[:CELL_NODES]

        if step == 0:
            for copy in ends:
                copy.wait_recv()
            for slot in (0, 1):
                side_mixed[slot, :SIDE], side_mixed[slot, SIDE:] = split(
                    mixed(ends_recv[slot, :, :DEPTH])[PROJECTORS * (1 - slot) : PROJECTORS * (1 - slot) + SIDE]
                )
            spread_mat[0] = jnp.concatenate([ends_recv[0, :, :DEPTH], own[0]], axis=0).astype(F32).T.astype(BF)
            spread_mat[1] = jnp.concatenate([own[1], ends_recv[1, :, :DEPTH]], axis=0).astype(F32).T.astype(BF)
            face_wide[0] = jnp.concatenate(
                [ends_recv[0, :, DEPTH:], ends_send[0, :, TAIL_COL:DEPTH]], axis=0
            ).astype(F32).T
            face_wide[1] = jnp.concatenate(
                [ends_send[1, :, :128], ends_recv[1, :, DEPTH:]], axis=0
            ).astype(F32).T
            skip = STRIDE - TAIL_COL
            face_mat[0] = face_wide[0, skip : skip + FACE_PAD, :].astype(BF)
            face_mat[1] = face_wide[1, :FACE_PAD, :].astype(BF)

        for copy in copies:
            copy.wait_recv()
        near = [near_recv.at[step, slot] for slot in (0, 1)]
        if step == 0:
            before, middle, after = whole_recv[0], weighted, whole_recv[1]
        else:
            before = sides[0] + near[0][own_part] + padded(far_recv[step - 1, 0], 1)
            middle = mine + padded(near[0][side_part], 1) + padded(near[1][side_part], 0)
            after = sides[1] + near[1][own_part] + padded(far_recv[step - 1, 1], 0)
            before, middle, after = before.astype(BF), middle.astype(BF), after.astype(BF)
        left = jnp.concatenate([before, middle], axis=0)
        right = jnp.concatenate([middle, after], axis=0)
        face = slice(COEFS, COEFS + FACE)
        target[:CELL_NODES, :] += gain * mm(spread_mat[0], left)[:CELL_NODES]
        target[STRIDE:NODE_DEV, :] += gain * mm(spread_mat[1], right)[:CELL_NODES]
        target[:FACE, :] += gain * (mm(face_mat[0], left)[:FACE] + near[0][face])
        target[NODE_DEV - FACE : NODE_DEV, :] += gain * (mm(face_mat[1], right)[:FACE] + near[1][face])

        if step < turns:
            pl.semaphore_wait(token_sems.at[step], 2)
            if step + 1 < turns:
                tell(step + 1)

    high, low = split(out_x[...] * out_x[...])
    loads[6].wait()
    weight = occ_ref[...] * (1.0 / (STATE_DEV * ns))
    weight_high = weight.astype(BF).astype(F32)
    row = lax.broadcasted_iota(jnp.int32, (16, STATE_DEV), 0)
    weights = jnp.where(row == 0, weight_high, jnp.where(row == 1, weight - weight_high, 0.0)).astype(BF)
    sums = mm_nt(weights, high) + mm_nt(weights, low)
    sums = sums[0:1] + sums[1:2]
    tiles = dens_send.shape[0]
    for tile in range(tiles):
        end = min(NODE_DEV, (tile + 1) * 128)
        dens_send[tile : tile + 1, : end - tile * 128] = sums[:, tile * 128 : end]
    dens_copies = []
    for shift in sorted(range(1, ns), key=lambda k: -min(k, ns - k)):
        dens_copies.append(send(dens_send, dens_recv.at[column], dens_sems, shift - 1, state_at(shift)))
    dens_recv[column] = dens_send[...]
    for copy in raw + ends + pending:
        copy.wait_send()
    for copy in dens_copies:
        copy.wait_recv()
    total = dens_recv[0]
    for peer in range(1, ns):
        total = total + dens_recv[peer]
    for tile in range(tiles):
        end = min(NODE_DEV, (tile + 1) * 128)
        out_d[tile * 128 : end] = total[tile, : end - tile * 128]
    for copy in dens_copies:
        copy.wait_send()


def solution(mesh):
    nc, ns = mesh.shape["cells"], mesh.shape["states"]

    def body(filter_input, cell_table, cell_type, atom_center, proj_values, coupling, occupation):
        any_space = pl.BlockSpec(memory_space=pl.ANY)
        vmem = pl.BlockSpec(memory_space=pltpu.VMEM)
        dma = pltpu.SemaphoreType.DMA
        filtered, density = pl.pallas_call(
            functools.partial(kernel, nc, ns),
            out_shape=(pltpu.VMEM((NODE_DEV, STATE_DEV), F32), pltpu.VMEM((NODE_DEV,), F32)),
            in_specs=[any_space] * 7,
            out_specs=(vmem, vmem),
            scratch_shapes=[
                pltpu.VMEM((NODE_DEV, STATE_DEV), BF),
                pltpu.VMEM((NODE_DEV - TAIL, STATE_DEV), BF),
                pltpu.VMEM((HEAD_ROWS, STATE_DEV), BF),
                pltpu.VMEM((CELL_NODES, NTYPE, CELL_NODES), BF),
                pltpu.SMEM(cell_type.shape, jnp.int32),
                pltpu.SMEM(atom_center.shape, jnp.int32),
                pltpu.VMEM(proj_values.shape, BF),
                pltpu.VMEM(coupling.shape, F32),
                pltpu.VMEM((1, STATE_DEV), F32),
                pltpu.VMEM((CELL_DEV, WIDE_ROWS, DEPTH), F32),
                pltpu.VMEM((CELL_DEV, ROWS, DEPTH), BF),
                pltpu.VMEM((2, COEFS, DEPTH), BF),
                pltpu.VMEM((CELL_DEV, COEFS, DEPTH), BF),
                pltpu.VMEM((CELL_DEV, 2 * COEFS, DEPTH), BF),
                pltpu.VMEM((2, 2 * COEFS, DEPTH), BF),
                pltpu.VMEM((2, 2 * SIDE, DEPTH), BF),
                pltpu.VMEM((2, COEFS, DEPTH + 128), BF),
                pltpu.VMEM((2, COEFS, DEPTH + 128), BF),
                pltpu.VMEM((2, DEPTH, 2 * COEFS), BF),
                pltpu.VMEM((2, 128, 2 * COEFS), F32),
                pltpu.VMEM((2, FACE_PAD, 2 * COEFS), BF),
                pltpu.VMEM((STEPS, FIELD, STATE_DEV), F32),
                pltpu.VMEM((STEPS, 2, NEAR_ROWS, STATE_DEV), F32),
                pltpu.VMEM((STEPS, 2, NEAR_ROWS, STATE_DEV), F32),
                pltpu.VMEM((STEPS - 1, 2, SIDE, STATE_DEV), F32),
                pltpu.VMEM((COEFS, STATE_DEV), BF),
                pltpu.VMEM((2, COEFS, STATE_DEV), BF),
                pltpu.VMEM((5, 128), F32),
                pltpu.VMEM((ns, 5, 128), F32),
                dma((7,)),
                dma((2, 2)),
                dma((2, 2)),
                dma((STEPS, 2, 2)),
                dma((2, 2)),
                dma((STEPS - 1, 2, 2)),
                dma((2, ns - 1)),
                pltpu.SemaphoreType.REGULAR((2,)),
            ],
            compiler_params=pltpu.CompilerParams(collective_id=0, has_side_effects=True),
        )(
            filter_input,
            jnp.swapaxes(cell_table, 0, 1),
            cell_type,
            atom_center,
            proj_values,
            coupling,
            occupation.reshape(1, STATE_DEV),
        )
        return filtered, density

    in_specs = (
        P("cells", "states"),
        P(),
        P("cells"),
        P("cells"),
        P("cells", None, None, None),
        P(),
        P("states"),
    )
    out_specs = (P("cells", "states"), P("cells"))
    return jax.shard_map(body, mesh=mesh, in_specs=in_specs, out_specs=out_specs, check_vma=False)
```

time: 54.5 us -> 49.7 us (0.912)
  Pallas kernels: 50.6 us -> 47.6 us
  local copies, waits for them, and re-layouts: 2.99 us -> 1.32 us
    pallas_call x1, Pallas kernels: 50.6 us -> 47.6 us  [body(): pl.pallas_call(functools.partial(kernel, nc, ns), out_shape=(pltpu.VMEM((...]
    unnamed x2, local copies, waits for them, and re-layouts: 2.99 us -> 1.32 us
where the time goes in v2:
time: 49.7 us; the launch traced here: 49.5 us
  Pallas kernels  47.6 us (96%)
  local copies, waits for them, and re-layouts  1.32 us (3%)
  between operations  0.64 us (1%)
    pallas_call x1, Pallas kernels, body(): pl.pallas_call(functools.partial(kernel, nc, ns), out_shape=(pltpu.VMEM((...  47.6 us
    unnamed x2, local copies, waits for them, and re-layouts  1.32 us

profile of v2, /device:TPU:1, one launch (start us, length us, event | category | flops | bytes accessed | tf_op | source)
XLA Modules:
  0.0 49.5 jit_solution(5815790549138056323)
XLA Ops:
  0.6 47.6 %shard_map.86 = (f32[637,128]{1,0:T(8,128)S(1)}, f32[637]{0:T(1024)S(1)}) custom-call(bf16[637,128]{1,0:T(8,128)(2,1)} %x_hbm.1, bf16[343,8,343]{2,1,0:T(8,128)(2,1)} %bitcast.2, s32[2]{0:T(128)} %type_hbm.1, s32[4]{0:T(128)} %center_hbm.1, bf16[4,3,16,343]{3,2,1,0:T(8,128)(2,1)} %proj_hbm.1, f32[16,16]{1,0:T(8,128)} %coup_hbm.1, f32[1,128]{1,0:T(1,128)} %bitcast.3), custom_call_target="tpu_custom_call" | custom-call | tf_op jit(solution)/shard_map/pallas_call | solution.py:391
  48.2 0.7 %copy.11 = f32[637,128]{1,0:T(8,128)} copy(f32[637,128]{1,0:T(8,128)S(1)} %get-tuple-element.2) | data formatting | bytes 652288
  49.0 0.6 %copy.12 = f32[637]{0:T(1024)} copy(f32[637]{0:T(1024)S(1)} %get-tuple-element.3) | data formatting | bytes 5096

commit v3 on v2

--- a/solution.py
+++ b/solution.py
@@ -25,13 +25,15 @@
 
 DEPTH = 384
 ROWS = 352
-WIDE_ROWS = 360
-FIELD = 688
+WIDE_ROWS = 368
+BLOCK = 640
+FIELD = 672
 TAIL = 288
 TAIL_SKIP = STRIDE - TAIL
 HEAD_ROWS = 344
 TAIL_COL = 256
 FACE_PAD = 56
+LAST_SKIP = NODE_DEV - FACE - (BLOCK - FACE_PAD)
 SIDE = COEFS - PROJECTORS
 NEAR_ROWS = COEFS + FACE_PAD + SIDE
 
@@ -88,17 +90,17 @@
     occ_ref,
     hwide,
     hmat,
-    hface,
     own,
-    own_mixed,
+    probe,
     edge_mixed,
-    side_mixed,
     ends_send,
     ends_recv,
+    spread_wide,
     spread_mat,
     face_wide,
     face_mat,
     field,
+    base_ref,
     near_send,
     near_recv,
     far_recv,
@@ -112,6 +114,8 @@
     near_sems,
     whole_sems,
     far_sems,
+    side_sems,
+    own_sems,
     dens_sems,
     token_sems,
 ):
@@ -194,6 +198,8 @@
 
     field[:, NODE_DEV - 5 :, :] = jnp.zeros((STEPS, FIELD - NODE_DEV + 5, STATE_DEV), F32)
     hwide[...] = jnp.zeros_like(hwide)
+    spread_wide[...] = jnp.zeros_like(spread_wide)
+    face_wide[...] = jnp.zeros_like(face_wide)
     dens_send[...] = jnp.zeros_like(dens_send)
     loads[2].wait()
     field[0, :NODE_DEV, :] = xin[...].astype(F32)
@@ -218,12 +224,16 @@
         half = both.shape[0] // 2
         return both[:half] + both[half:]
 
+    def moved(value, cell):
+        return pltpu.roll(value, TAIL_SKIP, 1) if cell else value
+
     for cell in range(CELL_DEV):
-        own_mixed[cell, :COEFS], own_mixed[cell, COEFS:] = split(mixed(own[cell]))
-    turned = pltpu.roll(mixed(ends_send[0, :, :DEPTH]), TAIL_SKIP, 1)
-    edge_mixed[0, :COEFS], edge_mixed[0, COEFS:] = split(turned)
-    edge_mixed[1, :COEFS], edge_mixed[1, COEFS:] = split(mixed(ends_send[1, :, :DEPTH]))
-
+        probe[cell, :COEFS], probe[cell, COEFS : 2 * COEFS] = split(moved(mixed(own[cell]), cell))
+        edge_mixed[cell, :COEFS], edge_mixed[cell, COEFS:] = split(
+            moved(mixed(ends_send[cell, :, :DEPTH]), 1 - cell)
+        )
+
+    faces = slice(2 * COEFS, 3 * COEFS)
     loads[4].wait()
     loads[5].wait()
     chunk = 256 // NTYPE
@@ -236,10 +246,15 @@
         entries = tab[start : start + count].reshape(count * NTYPE, CELL_NODES)
         rows = mm(take[:, : count * NTYPE], entries)
         for cell in range(CELL_DEV):
-            hwide[cell, start : start + count, :CELL_NODES] = rows[cell * chunk : cell * chunk + count]
+            begin = start + cell * TAIL_SKIP
+            hwide[cell, begin : begin + count, :CELL_NODES] = rows[cell * chunk : cell * chunk + count]
+    hwide[1] = moved(hwide[1], 1)
     hmat[...] = hwide[:, :ROWS].astype(BF)
-    hface[0] = hwide[0, :COEFS].astype(BF)
-    hface[1] = hwide[1, STRIDE : STRIDE + COEFS].astype(BF)
+    probe[1, faces] = hwide[1, STRIDE + TAIL_SKIP : STRIDE + TAIL_SKIP + COEFS].astype(BF)
+    hwide[0, LAST_SKIP : LAST_SKIP + FACE] = hwide[0, :FACE]
+    hwide[0, :LAST_SKIP] = jnp.zeros((LAST_SKIP, DEPTH), F32)
+    hwide[0, LAST_SKIP + FACE : COEFS] = jnp.zeros((COEFS - LAST_SKIP - FACE, DEPTH), F32)
+    probe[0, faces] = hwide[0, :COEFS].astype(BF)
 
     own_part = slice(0, COEFS)
     face_part = slice(COEFS, COEFS + FACE_PAD)
@@ -252,31 +267,29 @@
     pending = []
     for step, (gain, back) in enumerate(scales()):
         x = field.at[step]
-        cells = (x[:DEPTH, :].astype(BF), x[STRIDE : STRIDE + DEPTH, :].astype(BF))
-
-        mine = fold(mm(own_mixed[0], cells[0]) + mm(own_mixed[1], cells[1]))
+        rounded = x[...].astype(BF)
+        cells = (rounded[:DEPTH], rounded[TAIL:])
         copies = []
         sides = []
-        for slot, shift in ((0, -1), (1, 1)):
-            near_send[step, slot, face_part] = mm(hface[slot], cells[slot])[:FACE_PAD]
-            part = face_part
-            if step:
-                near_send[step, slot, own_part] = mine
-                side = fold(mm(side_mixed[slot], cells[slot]))
+
+        def exchange(part, sems):
+            rows = pl.ds(part.start, part.stop - part.start)
+            for slot, shift in ((0, -1), (1, 1)):
+                copies.append(
+                    send(
+                        near_send.at[step, slot, rows],
+                        near_recv.at[step, 1 - slot, rows],
+                        sems,
+                        slot,
+                        cell_at(shift),
+                    )
+                )
+
+        if step:
+            for slot, shift in ((0, -1), (1, 1)):
+                side = fold(mm(probe[slot, 3 * COEFS :], cells[slot]))
                 near_send[step, slot, side_part] = side
                 sides.append(padded(side, slot))
-                part = slice(0, NEAR_ROWS)
-            rows = pl.ds(part.start, part.stop - part.start)
-            copies.append(
-                send(
-                    near_send.at[step, slot, rows],
-                    near_recv.at[step, 1 - slot, rows],
-                    near_sems.at[step],
-                    slot,
-                    cell_at(shift),
-                )
-            )
-            if step:
                 copies.append(
                     send(
                         near_send.at[step, slot, pl.ds(side_part.start, SIDE)],
@@ -286,6 +299,15 @@
                         cell_at(2 * shift),
                     )
                 )
+            exchange(side_part, side_sems.at[step - 1])
+        mine = fold(mm(probe[0, : 2 * COEFS], cells[0]) + mm(probe[1, : 2 * COEFS], cells[1]))
+        if step:
+            for slot in (0, 1):
+                near_send[step, slot, own_part] = mine
+            exchange(own_part, own_sems.at[step - 1])
+        for slot in (0, 1):
+            near_send[step, slot, face_part] = mm(probe[slot, faces], cells[slot])[:FACE_PAD]
+        exchange(face_part, near_sems.at[step])
 
         if step == 0:
             for copy in raw:
@@ -300,33 +322,36 @@
             ]
         pending += copies
 
-        target = out_x if step == STEPS - 1 else field.at[step + 1]
         centre = (upper_edge + lower_edge) / 2.0
-        base = (-centre * gain) * x[:NODE_DEV, :]
+        base = (-centre * gain) * x[:BLOCK, :]
         if step:
-            base = base - back * field[step - 1, :NODE_DEV, :]
-        target[:NODE_DEV, :] = base
-        target[:CELL_NODES, :] += gain * mm(hmat[0], cells[0])[:CELL_NODES]
-        target[STRIDE:NODE_DEV, :] += gain * mm(hmat[1], cells[1])[:CELL_NODES]
+            base = base - back * field[step - 1, :BLOCK, :]
+        base_ref[...] = base
+        base_ref[:ROWS, :] += gain * mm(hmat[0], cells[0])
+        base_ref[TAIL:, :] += gain * mm(hmat[1], cells[1])
 
         if step == 0:
             for copy in ends:
                 copy.wait_recv()
             for slot in (0, 1):
-                side_mixed[slot, :SIDE], side_mixed[slot, SIDE:] = split(
-                    mixed(ends_recv[slot, :, :DEPTH])[PROJECTORS * (1 - slot) : PROJECTORS * (1 - slot) + SIDE]
-                )
-            spread_mat[0] = jnp.concatenate([ends_recv[0, :, :DEPTH], own[0]], axis=0).astype(F32).T.astype(BF)
-            spread_mat[1] = jnp.concatenate([own[1], ends_recv[1, :, :DEPTH]], axis=0).astype(F32).T.astype(BF)
-            face_wide[0] = jnp.concatenate(
-                [ends_recv[0, :, DEPTH:], ends_send[0, :, TAIL_COL:DEPTH]], axis=0
-            ).astype(F32).T
-            face_wide[1] = jnp.concatenate(
-                [ends_send[1, :, :128], ends_recv[1, :, DEPTH:]], axis=0
-            ).astype(F32).T
+                skip = PROJECTORS * (1 - slot)
+                side = moved(mixed(ends_recv[slot, :, :DEPTH])[skip : skip + SIDE], slot)
+                probe[slot, 3 * COEFS : 3 * COEFS + SIDE], probe[slot, 3 * COEFS + SIDE :] = split(side)
+            spread_wide[:DEPTH, : 2 * COEFS] = (
+                jnp.concatenate([ends_recv[0, :, :DEPTH], own[0]], axis=0).astype(F32).T
+            )
+            spread_wide[STRIDE : STRIDE + DEPTH, 2 * COEFS :] = (
+                jnp.concatenate([own[1], ends_recv[1, :, :DEPTH]], axis=0).astype(F32).T
+            )
+            spread_mat[...] = spread_wide[:BLOCK].astype(BF)
             skip = STRIDE - TAIL_COL
-            face_mat[0] = face_wide[0, skip : skip + FACE_PAD, :].astype(BF)
-            face_mat[1] = face_wide[1, :FACE_PAD, :].astype(BF)
+            face_wide[0, :128] = (
+                jnp.concatenate([ends_recv[0, :, DEPTH:], ends_send[0, :, TAIL_COL:DEPTH]], axis=0).astype(F32).T
+            )
+            ahead = jnp.concatenate([ends_send[1, :, :128], ends_recv[1, :, DEPTH:]], axis=0).astype(F32).T
+            face_wide[1, LAST_SKIP : LAST_SKIP + FACE] = ahead[:FACE]
+            face_mat[0] = face_wide[0, skip : skip + COEFS].astype(BF)
+            face_mat[1] = face_wide[1, :COEFS].astype(BF)
 
         for copy in copies:
             copy.wait_recv()
@@ -340,18 +365,31 @@
             before, middle, after = before.astype(BF), middle.astype(BF), after.astype(BF)
         left = jnp.concatenate([before, middle], axis=0)
         right = jnp.concatenate([middle, after], axis=0)
-        face = slice(COEFS, COEFS + FACE)
-        target[:CELL_NODES, :] += gain * mm(spread_mat[0], left)[:CELL_NODES]
-        target[STRIDE:NODE_DEV, :] += gain * mm(spread_mat[1], right)[:CELL_NODES]
-        target[:FACE, :] += gain * (mm(face_mat[0], left)[:FACE] + near[0][face])
-        target[NODE_DEV - FACE : NODE_DEV, :] += gain * (mm(face_mat[1], right)[:FACE] + near[1][face])
+        both = jnp.concatenate([left, right], axis=0)
+        half = BLOCK // 2
+        spread = jnp.concatenate([mm(spread_mat[:half], both), mm(spread_mat[half:], both)], axis=0)
+        top = mm(face_mat[0], left)[:FACE_PAD] + near[0][face_part]
+        bottom = mm(face_mat[1], right)[:FACE_PAD] + near[1][face_part]
+        spread = jnp.concatenate(
+            [
+                spread[:FACE_PAD] + top,
+                spread[FACE_PAD : BLOCK - FACE_PAD],
+                spread[BLOCK - FACE_PAD :] + bottom,
+            ],
+            axis=0,
+        )
+        following = base_ref[...] + gain * spread
+        if step < STEPS - 1:
+            field[step + 1, :BLOCK, :] = following
+        else:
+            out_x[...] = following[:NODE_DEV]
 
         if step < turns:
             pl.semaphore_wait(token_sems.at[step], 2)
             if step + 1 < turns:
                 tell(step + 1)
 
-    high, low = split(out_x[...] * out_x[...])
+    high, low = split(following * following)
     loads[6].wait()
     weight = occ_ref[...] * (1.0 / (STATE_DEV * ns))
     weight_high = weight.astype(BF).astype(F32)
@@ -381,6 +419,17 @@
         copy.wait_send()
 
 
+def store(x_ref, d_ref, x_hbm, d_hbm, sem):
+    copies = [
+        pltpu.make_async_copy(x_ref, x_hbm, sem.at[0]),
+        pltpu.make_async_copy(d_ref, d_hbm, sem.at[1]),
+    ]
+    for copy in copies:
+        copy.start()
+    for copy in copies:
+        copy.wait()
+
+
 def solution(mesh):
     nc, ns = mesh.shape["cells"], mesh.shape["states"]
 
@@ -405,17 +454,17 @@
                 pltpu.VMEM((1, STATE_DEV), F32),
                 pltpu.VMEM((CELL_DEV, WIDE_ROWS, DEPTH), F32),
                 pltpu.VMEM((CELL_DEV, ROWS, DEPTH), BF),
-                pltpu.VMEM((2, COEFS, DEPTH), BF),
                 pltpu.VMEM((CELL_DEV, COEFS, DEPTH), BF),
-                pltpu.VMEM((CELL_DEV, 2 * COEFS, DEPTH), BF),
+                pltpu.VMEM((CELL_DEV, 3 * COEFS + 2 * SIDE, DEPTH), BF),
                 pltpu.VMEM((2, 2 * COEFS, DEPTH), BF),
-                pltpu.VMEM((2, 2 * SIDE, DEPTH), BF),
                 pltpu.VMEM((2, COEFS, DEPTH + 128), BF),
                 pltpu.VMEM((2, COEFS, DEPTH + 128), BF),
-                pltpu.VMEM((2, DEPTH, 2 * COEFS), BF),
+                pltpu.VMEM((STRIDE + DEPTH + 2, 4 * COEFS), F32),
+                pltpu.VMEM((BLOCK, 4 * COEFS), BF),
                 pltpu.VMEM((2, 128, 2 * COEFS), F32),
-                pltpu.VMEM((2, FACE_PAD, 2 * COEFS), BF),
+                pltpu.VMEM((2, COEFS, 2 * COEFS), BF),
                 pltpu.VMEM((STEPS, FIELD, STATE_DEV), F32),
+                pltpu.VMEM((BLOCK, STATE_DEV), F32),
                 pltpu.VMEM((STEPS, 2, NEAR_ROWS, STATE_DEV), F32),
                 pltpu.VMEM((STEPS, 2, NEAR_ROWS, STATE_DEV), F32),
                 pltpu.VMEM((STEPS - 1, 2, SIDE, STATE_DEV), F32),
@@ -428,6 +477,8 @@
                 dma((2, 2)),
                 dma((STEPS, 2, 2)),
                 dma((2, 2)),
+                dma((STEPS - 1, 2, 2)),
+                dma((STEPS - 1, 2, 2)),
                 dma((STEPS - 1, 2, 2)),
                 dma((2, ns - 1)),
                 pltpu.SemaphoreType.REGULAR((2,)),
@@ -442,7 +493,16 @@
             coupling,
             occupation.reshape(1, STATE_DEV),
         )
-        return filtered, density
+        return pl.pallas_call(
+            store,
+            out_shape=(
+                jax.ShapeDtypeStruct((NODE_DEV, STATE_DEV), F32),
+                jax.ShapeDtypeStruct((NODE_DEV,), F32),
+            ),
+            in_specs=[any_space, any_space],
+            out_specs=(any_space, any_space),
+            scratch_shapes=[dma((2,))],
+        )(*(pltpu.with_memory_space_constraint(v, pltpu.VMEM) for v in (filtered, density)))
 
     in_specs = (
         P("cells", "states"),

time: 49.7 us -> 48.7 us (0.980)
  local copies, waits for them, and re-layouts: 1.32 us -> 0 us
    unnamed x2 -> x0, local copies, waits for them, and re-layouts: 1.32 us -> none
    pallas_call x0 -> x1, Pallas kernels: none -> 0.75 us  [body(): pl.pallas_call(store, out_shape=(jax.ShapeDtypeStruct((NODE_DEV, STATE_DE...]
where the time goes in v3:
time: 48.7 us; the launch traced here: 48.6 us
  Pallas kernels  47.9 us (98%)
  between operations  0.64 us (1%)
    pallas_call x1, Pallas kernels, body(): pl.pallas_call(functools.partial(kernel, nc, ns), out_shape=(pltpu.VMEM((...  47.2 us

profile of v3, /device:TPU:1, one launch (start us, length us, event | category | flops | bytes accessed | tf_op | source)
XLA Modules:
  0.0 48.6 jit_solution(10651035062186597575)
XLA Ops:
  0.6 47.2 %shard_map.86 = (f32[637,128]{1,0:T(8,128)S(1)}, f32[637]{0:T(1024)S(1)}) custom-call(bf16[637,128]{1,0:T(8,128)(2,1)} %x_hbm.1, bf16[343,8,343]{2,1,0:T(8,128)(2,1)} %bitcast.2, s32[2]{0:T(128)} %type_hbm.1, s32[4]{0:T(128)} %center_hbm.1, bf16[4,3,16,343]{3,2,1,0:T(8,128)(2,1)} %proj_hbm.1, f32[16,16]{1,0:T(8,128)} %coup_hbm.1, f32[1,128]{1,0:T(1,128)} %bitcast.3), custom_call_target="tpu_custom_call" | custom-call | tf_op jit(solution)/shard_map/pallas_call | solution.py:440
  47.8 0.7 %shard_map.87 = (f32[637,128]{1,0:T(8,128)}, f32[637]{0:T(1024)}) custom-call(f32[637,128]{1,0:T(8,128)S(1)} %get-tuple-element.4.x_ref, f32[637]{0:T(1024)S(1)} %get-tuple-element.5.d_ref), custom_call_target="tpu_custom_call" | custom-call | tf_op jit(solution)/shard_map/pallas_call | solution.py:496

commit v4 on v3

--- a/solution.py
+++ b/solution.py
@@ -265,9 +265,9 @@
         return jnp.concatenate([side, blank] if slot else [blank, side], axis=0)
 
     pending = []
+    rounded = field[0].astype(BF)
     for step, (gain, back) in enumerate(scales()):
         x = field.at[step]
-        rounded = x[...].astype(BF)
         cells = (rounded[:DEPTH], rounded[TAIL:])
         copies = []
         sides = []
@@ -285,7 +285,11 @@
                     )
                 )
 
+        mine = fold(mm(probe[0, : 2 * COEFS], cells[0]) + mm(probe[1, : 2 * COEFS], cells[1]))
         if step:
+            for slot in (0, 1):
+                near_send[step, slot, own_part] = mine
+            exchange(own_part, own_sems.at[step - 1])
             for slot, shift in ((0, -1), (1, 1)):
                 side = fold(mm(probe[slot, 3 * COEFS :], cells[slot]))
                 near_send[step, slot, side_part] = side
@@ -300,11 +304,6 @@
                     )
                 )
             exchange(side_part, side_sems.at[step - 1])
-        mine = fold(mm(probe[0, : 2 * COEFS], cells[0]) + mm(probe[1, : 2 * COEFS], cells[1]))
-        if step:
-            for slot in (0, 1):
-                near_send[step, slot, own_part] = mine
-            exchange(own_part, own_sems.at[step - 1])
         for slot in (0, 1):
             near_send[step, slot, face_part] = mm(probe[slot, faces], cells[slot])[:FACE_PAD]
         exchange(face_part, near_sems.at[step])
@@ -321,6 +320,10 @@
                 for slot, shift in ((0, -1), (1, 1))
             ]
         pending += copies
+        if step == 1 and turns > 0:
+            pl.semaphore_wait(token_sems.at[0], 2)
+            if turns > 1:
+                tell(1)
 
         centre = (upper_edge + lower_edge) / 2.0
         base = (-centre * gain) * x[:BLOCK, :]
@@ -381,13 +384,9 @@
         following = base_ref[...] + gain * spread
         if step < STEPS - 1:
             field[step + 1, :BLOCK, :] = following
+            rounded = jnp.concatenate([following.astype(BF), jnp.zeros((FIELD - BLOCK, STATE_DEV), BF)], axis=0)
         else:
             out_x[...] = following[:NODE_DEV]
-
-        if step < turns:
-            pl.semaphore_wait(token_sems.at[step], 2)
-            if step + 1 < turns:
-                tell(step + 1)
 
     high, low = split(following * following)
     loads[6].wait()
@@ -401,6 +400,8 @@
     for tile in range(tiles):
         end = min(NODE_DEV, (tile + 1) * 128)
         dens_send[tile : tile + 1, : end - tile * 128] = sums[:, tile * 128 : end]
+    if turns > 1:
+        pl.semaphore_wait(token_sems.at[1], 2)
     dens_copies = []
     for shift in sorted(range(1, ns), key=lambda k: -min(k, ns - k)):
         dens_copies.append(send(dens_send, dens_recv.at[column], dens_sems, shift - 1, state_at(shift)))

time: 48.7 us -> 48.5 us (level)
  no operation moved by 1% of the time
where the time goes in v4:
time: 48.5 us; the launch traced here: 48.3 us
  Pallas kernels  47.7 us (98%)
  between operations  0.64 us (1%)
    pallas_call x1, Pallas kernels, body(): pl.pallas_call(functools.partial(kernel, nc, ns), out_shape=(pltpu.VMEM((...  47 us

profile of v4, /device:TPU:1, one launch (start us, length us, event | category | flops | bytes accessed | tf_op | source)
XLA Modules:
  0.0 48.3 jit_solution(3134633559433284242)
XLA Ops:
  0.6 47.0 %shard_map.86 = (f32[637,128]{1,0:T(8,128)S(1)}, f32[637]{0:T(1024)S(1)}) custom-call(bf16[637,128]{1,0:T(8,128)(2,1)} %x_hbm.1, bf16[343,8,343]{2,1,0:T(8,128)(2,1)} %bitcast.2, s32[2]{0:T(128)} %type_hbm.1, s32[4]{0:T(128)} %center_hbm.1, bf16[4,3,16,343]{3,2,1,0:T(8,128)(2,1)} %proj_hbm.1, f32[16,16]{1,0:T(8,128)} %coup_hbm.1, f32[1,128]{1,0:T(1,128)} %bitcast.3), custom_call_target="tpu_custom_call" | custom-call | tf_op jit(solution)/shard_map/pallas_call | solution.py:441
  47.6 0.7 %shard_map.87 = (f32[637,128]{1,0:T(8,128)}, f32[637]{0:T(1024)}) custom-call(f32[637,128]{1,0:T(8,128)S(1)} %get-tuple-element.4.x_ref, f32[637]{0:T(1024)S(1)} %get-tuple-element.5.d_ref), custom_call_target="tpu_custom_call" | custom-call | tf_op jit(solution)/shard_map/pallas_call | solution.py:497

commit v5 on v4

--- a/solution.py
+++ b/solution.py
@@ -115,7 +115,6 @@
     whole_sems,
     far_sems,
     side_sems,
-    own_sems,
     dens_sems,
     token_sems,
 ):
@@ -270,11 +269,10 @@
         x = field.at[step]
         cells = (rounded[:DEPTH], rounded[TAIL:])
         copies = []
-        sides = []
 
         def exchange(part, sems):
             rows = pl.ds(part.start, part.stop - part.start)
-            for slot, shift in ((0, -1), (1, 1)):
+            for slot, shift in ((1, 1), (0, -1)):
                 copies.append(
                     send(
                         near_send.at[step, slot, rows],
@@ -285,15 +283,12 @@
                     )
                 )
 
-        mine = fold(mm(probe[0, : 2 * COEFS], cells[0]) + mm(probe[1, : 2 * COEFS], cells[1]))
+        sides = [None, None]
         if step:
-            for slot in (0, 1):
-                near_send[step, slot, own_part] = mine
-            exchange(own_part, own_sems.at[step - 1])
-            for slot, shift in ((0, -1), (1, 1)):
+            for slot, shift in ((1, 1), (0, -1)):
                 side = fold(mm(probe[slot, 3 * COEFS :], cells[slot]))
                 near_send[step, slot, side_part] = side
-                sides.append(padded(side, slot))
+                sides[slot] = padded(side, slot)
                 copies.append(
                     send(
                         near_send.at[step, slot, pl.ds(side_part.start, SIDE)],
@@ -304,9 +299,13 @@
                     )
                 )
             exchange(side_part, side_sems.at[step - 1])
+        mine = fold(mm(probe[0, : 2 * COEFS], cells[0]) + mm(probe[1, : 2 * COEFS], cells[1]))
+        if step:
+            for slot in (0, 1):
+                near_send[step, slot, own_part] = mine
         for slot in (0, 1):
             near_send[step, slot, face_part] = mm(probe[slot, faces], cells[slot])[:FACE_PAD]
-        exchange(face_part, near_sems.at[step])
+        exchange(slice(0, face_part.stop) if step else face_part, near_sems.at[step])
 
         if step == 0:
             for copy in raw:
@@ -480,7 +479,6 @@
                 dma((2, 2)),
                 dma((STEPS - 1, 2, 2)),
                 dma((STEPS - 1, 2, 2)),
-                dma((STEPS - 1, 2, 2)),
                 dma((2, ns - 1)),
                 pltpu.SemaphoreType.REGULAR((2,)),
             ],

time: 48.5 us -> 48.5 us (level)
  no operation moved by 1% of the time
where the time goes in v5:
time: 48.5 us; the launch traced here: 48.4 us
  Pallas kernels  47.7 us (98%)
  between operations  0.64 us (1%)
    pallas_call x1, Pallas kernels, body(): pl.pallas_call(functools.partial(kernel, nc, ns), out_shape=(pltpu.VMEM((...  47 us

profile of v5, /device:TPU:1, one launch (start us, length us, event | category | flops | bytes accessed | tf_op | source)
XLA Modules:
  0.0 48.4 jit_solution(16000330869168781874)
XLA Ops:
  0.6 47.0 %shard_map.86 = (f32[637,128]{1,0:T(8,128)S(1)}, f32[637]{0:T(1024)S(1)}) custom-call(bf16[637,128]{1,0:T(8,128)(2,1)} %x_hbm.1, bf16[343,8,343]{2,1,0:T(8,128)(2,1)} %bitcast.2, s32[2]{0:T(128)} %type_hbm.1, s32[4]{0:T(128)} %center_hbm.1, bf16[4,3,16,343]{3,2,1,0:T(8,128)(2,1)} %proj_hbm.1, f32[16,16]{1,0:T(8,128)} %coup_hbm.1, f32[1,128]{1,0:T(1,128)} %bitcast.3), custom_call_target="tpu_custom_call" | custom-call | tf_op jit(solution)/shard_map/pallas_call | solution.py:440
  47.6 0.7 %shard_map.87 = (f32[637,128]{1,0:T(8,128)}, f32[637]{0:T(1024)}) custom-call(f32[637,128]{1,0:T(8,128)S(1)} %get-tuple-element.4.x_ref, f32[637]{0:T(1024)S(1)} %get-tuple-element.5.d_ref), custom_call_target="tpu_custom_call" | custom-call | tf_op jit(solution)/shard_map/pallas_call | solution.py:495

commit v6 on v5

--- a/solution.py
+++ b/solution.py
@@ -152,8 +152,8 @@
 
     pl.semaphore_wait(barrier, 4)
     raw = [
+        send(x_hbm.at[pl.ds(TAIL, NODE_DEV - TAIL)], x_left, raw_sems, 1, cell_at(1)),
         send(x_hbm.at[pl.ds(0, HEAD_ROWS)], x_right, raw_sems, 0, cell_at(-1)),
-        send(x_hbm.at[pl.ds(TAIL, NODE_DEV - TAIL)], x_left, raw_sems, 1, cell_at(1)),
     ]
 
     def tell(turn):
@@ -191,8 +191,8 @@
     ends_send[0, :, DEPTH:] = own[0, :, :128]
     ends_send[1, :, DEPTH:] = own[1, :, TAIL_COL:]
     ends = [
+        send(ends_send.at[1], ends_recv.at[0], ends_sems, 1, cell_at(1)),
         send(ends_send.at[0], ends_recv.at[1], ends_sems, 0, cell_at(-1)),
-        send(ends_send.at[1], ends_recv.at[0], ends_sems, 1, cell_at(1)),
     ]
 
     field[:, NODE_DEV - 5 :, :] = jnp.zeros((STEPS, FIELD - NODE_DEV + 5, STATE_DEV), F32)
@@ -316,7 +316,7 @@
             whole_send[...] = weighted
             copies += [
                 send(whole_send, whole_recv.at[1 - slot], whole_sems, slot, cell_at(shift))
-                for slot, shift in ((0, -1), (1, 1))
+                for slot, shift in ((1, 1), (0, -1))
             ]
         pending += copies
         if step == 1 and turns > 0:

time: 48.5 us -> 48.5 us (level)
  no operation moved by 1% of the time
where the time goes in v6:
time: 48.5 us; the launch traced here: 48.4 us
  Pallas kernels  47.7 us (98%)
  between operations  0.64 us (1%)
    pallas_call x1, Pallas kernels, body(): pl.pallas_call(functools.partial(kernel, nc, ns), out_shape=(pltpu.VMEM((...  47 us

profile of v6, /device:TPU:1, one launch (start us, length us, event | category | flops | bytes accessed | tf_op | source)
XLA Modules:
  0.0 48.4 jit_solution(6635619219963769378)
XLA Ops:
  0.6 47.0 %shard_map.86 = (f32[637,128]{1,0:T(8,128)S(1)}, f32[637]{0:T(1024)S(1)}) custom-call(bf16[637,128]{1,0:T(8,128)(2,1)} %x_hbm.1, bf16[343,8,343]{2,1,0:T(8,128)(2,1)} %bitcast.2, s32[2]{0:T(128)} %type_hbm.1, s32[4]{0:T(128)} %center_hbm.1, bf16[4,3,16,343]{3,2,1,0:T(8,128)(2,1)} %proj_hbm.1, f32[16,16]{1,0:T(8,128)} %coup_hbm.1, f32[1,128]{1,0:T(1,128)} %bitcast.3), custom_call_target="tpu_custom_call" | custom-call | tf_op jit(solution)/shard_map/pallas_call | solution.py:440
  47.6 0.7 %shard_map.87 = (f32[637,128]{1,0:T(8,128)}, f32[637]{0:T(1024)}) custom-call(f32[637,128]{1,0:T(8,128)S(1)} %get-tuple-element.4.x_ref, f32[637]{0:T(1024)S(1)} %get-tuple-element.5.d_ref), custom_call_target="tpu_custom_call" | custom-call | tf_op jit(solution)/shard_map/pallas_call | solution.py:495
